TPU v7x, 32 devices: a whole 2x2x4 slice. The times are simulated.
32 devices in a mesh: section: 2 (over x), expert: 16 (over z, y, core).
Axes of the slice: x: 2, y: 2, z: 4, core: 2. Of those that a mesh axis runs over, the one named last changes fastest.
Arguments:
- tokens: bfloat16 [2, 256, 2048], P('section', 'expert'), may hold values from -6 to 6
- out_grad: bfloat16 [2, 256, 2048], P('section', 'expert'), may hold values from -1 to 1
- expert_ids: int32 [2, 256, 2], P('section'), may hold values from 0 to 3, all different within a row; in each aligned block of 16 rows (0 to 15, 16 to 31, ..., all dimensions but the last counted through in order) at most 14 rows name the same one
- gate_weights: bfloat16 [2, 256, 2], P('section'), may hold values from 0.049804688 to 1
- gate_up_rows: bfloat16 [2, 16, 384, 2048], P('section', 'expert'), may hold values from -0.125 to 0.125
- down_rows: bfloat16 [2, 16, 192, 2048], P('section', 'expert'), may hold values from -0.21875 to 0.21875
Outputs:
- gate_grad: float32 [2, 256, 2], P('section', 'expert')
- handed: bfloat16 [2, 256, 2048], P('section', 'expert')
Inputs may be any that keep to these rules, and one draw needn't show every extreme that they name: `expert_ids`: within the rows of one device (16 consecutive rows of a section), every expert id appears in at most 14 rows, and some id reaches 14; the 2 ids of a row are distinct.
All inputs are finite; a program needn't handle non-finite values.
Results may differ from a plain program's by a relative error of at most 0.0049.
Values may be sent and summed in bfloat16 or wider, within the bound.
No kernel may reach another device: no remote copies, remote signals or barrier semaphores. Data moves between devices by JAX's collectives and lax.ppermute only.
A program may use at most 64 MiB of HBM per device.

v0:
```python
import jax
import jax.numpy as jnp
from jax import lax
from jax.sharding import PartitionSpec as P


def from_behind(shard, axis, by):
    length = lax.axis_size(axis)
    pairs = [(i, i + by) for i in range(length) if 0 <= i + by < length]
    return lax.ppermute(shard, axis, pairs)


def slot_table(matches, capacity):
    ranked = jnp.cumsum(matches, axis=-1) - 1.0
    levels = jnp.arange(capacity, dtype=jnp.float32)
    return matches[..., None, :] * (ranked[..., None, :] == levels[:, None]).astype(jnp.float32)


def expert_grads(rows_in, rows_grad, slot_gate, gate_up, down_mat):
    width = down_mat.shape[0]
    contract = (((1,), (1,)), ((), ()))
    both = lax.dot_general(rows_in, gate_up, contract, preferred_element_type=jnp.float32)
    first = both[:, :width]
    second = both[:, width:]
    back = lax.dot_general(rows_grad, down_mat, contract, preferred_element_type=jnp.float32)
    sigma = jax.nn.sigmoid(first)
    active = first * sigma
    slot_grad = jnp.sum(back * active * second, axis=1)
    scaled = slot_gate[:, None] * back
    d_first = scaled * second * sigma * (1.0 + first * (1.0 - sigma))
    d_second = scaled * active
    d_both = jnp.concatenate([d_first, d_second], axis=1).astype(jnp.bfloat16)
    contrib = jnp.dot(d_both, gate_up, preferred_element_type=jnp.float32)
    return (contrib, slot_grad)


def body(tokens, out_grad, expert_ids, gate_weights, gate_up_rows, down_rows):
    group_size = lax.axis_size("expert")
    expert_count = max(2, group_size // 4)
    part_count = group_size // expert_count
    position = lax.axis_index("expert")
    my_expert = position // part_count
    block_rows = tokens.shape[1]
    model_width = tokens.shape[2]
    route_count = expert_ids.shape[2]
    pairs = block_rows * route_count
    capacity = min(block_rows, max(2, 7 * block_rows * route_count // (4 * expert_count)))
    gate_up = gate_up_rows[0, 0]
    down_mat = down_rows[0, 0]
    all_ids = expert_ids[0]
    all_gates = gate_weights[0].astype(jnp.float32)
    highest = lax.Precision.HIGHEST
    all_in, all_grad = (
        lax.all_gather(tokens[0], "expert", axis=0, tiled=True),
        lax.all_gather(out_grad[0], "expert", axis=0, tiled=True),
    )
    matches = (all_ids.reshape(group_size, pairs) == my_expert).astype(jnp.float32)
    slot_pick = slot_table(matches, capacity)
    chooser = slot_pick.reshape(group_size, capacity, block_rows, route_count).sum(axis=-1)
    slot_gate = jnp.sum(slot_pick * all_gates.reshape(group_size, 1, pairs), axis=-1)
    chooser_half = chooser.astype(jnp.bfloat16)
    rows_in = jnp.einsum(
        "jrt,jtd->jrd",
        chooser_half,
        all_in.reshape(group_size, block_rows, model_width),
        preferred_element_type=jnp.float32,
    ).astype(jnp.bfloat16)
    rows_grad = jnp.einsum(
        "jrt,jtd->jrd",
        chooser_half,
        all_grad.reshape(group_size, block_rows, model_width),
        preferred_element_type=jnp.float32,
    ).astype(jnp.bfloat16)
    contrib, slot_grad = expert_grads(
        rows_in.reshape(-1, model_width),
        rows_grad.reshape(-1, model_width),
        slot_gate.reshape(-1),
        gate_up,
        down_mat,
    )
    partial_value = jnp.einsum(
        "jrt,jrd->jtd",
        chooser,
        contrib.reshape(group_size, capacity, model_width),
        precision=highest,
    ).reshape(group_size * block_rows, model_width)
    gate_part = jnp.einsum(
        "jrp,jr->jp", slot_pick, slot_grad.reshape(group_size, capacity), precision=highest
    ).reshape(group_size * block_rows, route_count)
    grad_rows, gate_grad = (
        lax.psum_scatter(partial_value, "expert", scatter_dimension=0, tiled=True),
        lax.psum_scatter(gate_part, "expert", scatter_dimension=0, tiled=True),
    )
    handed = from_behind(grad_rows.astype(jnp.bfloat16), "section", -1)
    return (gate_grad[None], handed[None])


def solution(mesh):
    return jax.shard_map(
        body,
        mesh=mesh,
        in_specs=(
            P("section", "expert", None),
            P("section", "expert", None),
            P("section", None, None),
            P("section", None, None),
            P("section", "expert", None, None),
            P("section", "expert", None, None),
        ),
        out_specs=(P("section", "expert", None), P("section", "expert", None)),
        check_vma=False,
    )
```

profile of v0, /device:TPU:0, one launch (start us, length us, event | category | flops | bytes accessed | tf_op | source)
XLA Modules:
  0.0 227.0 jit_solution(1445343976378787823)
XLA Ops:
  7.2 0.7 all-gather.7.cloned.1.call-update
  8.0 0.7 all-gather.5.cloned.1.call-update
  8.7 0.7 compare_convert_fusion
  9.5 0.1 copy.39
  9.6 0.1 reshape.91
  9.7 0.1 reshape.90
  9.9 0.2 reduce_window_sum.11
  10.3 0.6 copy-done.1
  10.9 0.8 copy.48
  11.8 0.1 reshape.93
  11.9 0.7 multiply_reduce_fusion.1
  12.7 38.2 %all-gather.7.cloned.1.call-done = bf16[1,256,2048]{2,1,0:T(8,128)(2,1)} async-done(((bf16[1,16,2048]{2,1,0:T(8,128)(2,1)}), bf16[1,256,2048]{2,1,0:T(8,128)(2,1)}) %all-gather.7.cloned.1.call-update) | async-done | bytes 1048592 | tf_op jit(solution)/shard_map/all_gather | solution.py:54
  50.9 1.6 convolution_convert_fusion
  52.5 0.3 reshape.86
  52.8 37.1 %all-gather.5.cloned.1.call-done = bf16[1,256,2048]{2,1,0:T(8,128)(2,1)} async-done(((bf16[1,16,2048]{2,1,0:T(8,128)(2,1)}), bf16[1,256,2048]{2,1,0:T(8,128)(2,1)}) %all-gather.5.cloned.1.call-update) | async-done | bytes 1048592 | tf_op jit(solution)/shard_map/all_gather | solution.py:55
  89.9 1.7 convolution_convert_fusion.1
  91.6 1.2 reshape.84
  92.8 0.6 fusion.2
  93.4 0.6 copy-done.3
  94.0 0.2 copy-done.6
  94.2 0.5 multiply_convert_fusion.1
  94.7 0.1 copy.50
  95.0 0.7 fusion
  95.8 3.3 %fusion.12 = f32[16,16,2048]{2,1,0:T(8,128)} fusion(f32[16,14,2048]{2,1,0:T(8,128)S(1)} %fusion, f32[16,14,16]{2,0,1:T(8,128)S(1)} %copy-done.2), kind=kOutput, calls=%fused_computation.20 | convolution fusion | flops 88080384 | bytes 3946496 | tf_op jit(solution)/shard_map/jrt,jrd->jtd/dot_general | solution.py:81
  99.3 60.5 %reduce-scatter.5.cloned.1.call-done = f32[16,2048]{1,0:T(8,128)} async-done(((f32[256,2048]{1,0:T(8,128)}), f32[16,2048]{1,0:T(8,128)}) %reduce-scatter.5.cloned.1.call-update) | async-done | bytes 131088 | tf_op jit(solution)/shard_map/reduce_scatter | solution.py:91
  159.8 0.9 convert_element_type.62
  160.7 1.3 collective-permute-start
  162.0 0.3 fusion.10
  162.3 0.7 reshape.88
  163.1 55.4 %reduce-scatter.3.cloned.1.call-done = f32[16,2]{1,0:T(8,128)} async-done(((f32[256,2]{1,0:T(8,128)}), f32[16,2]{1,0:T(8,128)}) %reduce-scatter.3.cloned.1.call-update) | async-done | bytes 144 | tf_op jit(solution)/shard_map/reduce_scatter | solution.py:92
  218.5 1.3 copy.47
  219.8 0.6 copy.66
  (30 shorter events, 1.0 us)
Async XLA Ops:
  7.2 85.6 %copy-start = (bf16[1,1,384,2048]{3,2,1,0:T(8,128)(2,1)S(1)}, bf16[1,1,384,2048]{3,2,1,0:T(8,128)(2,1)}, u32[]{:S(2)}) copy-start(bf16[1,1,384,2048]{3,2,1,0:T(8,128)(2,1)} %param.10) | copy-start | bytes 4718596
  7.2 43.7 %all-gather.7.cloned.1.call-start = ((), (), s32[]{:S(2)}) async-start(), calls=%async_computation.5 | async-start | bytes 1114112 | tf_op jit(solution)/shard_map/all_gather | solution.py:54
  7.9 82.0 %all-gather.5.cloned.1.call-start = ((), (), s32[]{:S(2)}) async-start(), calls=%async_computation.4 | async-start | bytes 1114112 | tf_op jit(solution)/shard_map/all_gather | solution.py:55
  8.7 151.2 %reduce-scatter.5.cloned.1.call-start = ((), (), s32[]{:S(2)}) async-start(), calls=%async_computation.3 | async-start | bytes 2228224 | tf_op jit(solution)/shard_map/reduce_scatter | solution.py:91
  10.3 0.7 copy-start.1
  10.9 39.9 %copy-start.4 = (bf16[16,14,16]{2,0,1:T(8,128)(2,1)}, bf16[16,14,16]{2,0,1:T(8,128)(2,1)S(1)}, u32[]{:S(2)}) copy-start(bf16[16,14,16]{2,0,1:T(8,128)(2,1)S(1)} %convert_element_type.57) | copy-start | bytes 21508
  92.8 1.2 copy-start.3
  92.8 1.4 copy-start.6
  94.9 0.9 copy-start.2
  99.1 62.9 %copy-start.5 = (f32[16,14,32]{2,0,1:T(8,128)S(1)}, f32[16,14,32]{2,0,1:T(8,128)}, u32[]{:S(2)}) copy-start(f32[16,14,32]{2,0,1:T(8,128)} %get-tuple-element.6) | copy-start | bytes 86020
  99.2 119.3 %reduce-scatter.3.cloned.1.call-start = ((), (), s32[]{:S(2)}) async-start(), calls=%async_computation.2 | async-start | bytes 139264 | tf_op jit(solution)/shard_map/reduce_scatter | solution.py:92
  160.7 59.1 %collective-permute-start = (bf16[16,2048]{1,0:T(8,128)(2,1)S(1)}, bf16[16,2048]{1,0:T(8,128)(2,1)S(1)}, u32[]{:S(2)}, u32[]{:S(2)}) collective-permute-start(bf16[16,2048]{1,0:T(8,128)(2,1)S(1)} %convert_element_type.62), channel_id=1, source_target_pairs={{16,0},{17,1},{18,2},{19,3},{20,4},{21,5},{22,6},{23,7},{24,8},{25... | collective-permute-start | bytes 196616 | tf_op jit(solution)/shard_map/ppermute | solution.py:10
Sparse Core Ops, SparseCore 0:
  10.2 40.6 all-gather.6
  53.0 36.8 all-gather.4
  99.3 60.4 reduce-scatter.4
  163.5 54.9 reduce-scatter.2
where the time goes:
time: 227 us
  waiting for transfers between devices  193 us (85%)
  between operations  13.9 us (6%)
  matrix products  8.71 us (4%)
  local copies, waits for them, and re-layouts  7.79 us (3%)
  other arithmetic  2.49 us (1%)
    reduce_scatter x1, waiting for transfers between devices, body(): lax.psum_scatter(partial_value, 'expert', scatter_dimension=0, tiled=True)  60.5 us
    reduce_scatter x1, waiting for transfers between devices, body(): lax.psum_scatter(gate_part, 'expert', scatter_dimension=0, tiled=True)  55.4 us
    all_gather x1, waiting for transfers between devices, body(): lax.all_gather(tokens[0], 'expert', axis=0, tiled=True)  38.2 us
    all_gather x1, waiting for transfers between devices, body(): lax.all_gather(out_grad[0], 'expert', axis=0, tiled=True)  37.1 us
  transfers between devices with their start and end apart: 5, of which 4 were waited for; matrix products, arithmetic and copies ran while one was open for 3% of the time, Pallas kernels for 0%

commit v1 on v0

v1 whole, which is shorter than its diff:
```python
import functools

import jax
import jax.numpy as jnp
from jax import lax
from jax.experimental import pallas as pl
from jax.experimental.pallas import tpu as pltpu
from jax.sharding import PartitionSpec as P

PAD = 128


def locate(position):
    return position // 4, position // 2 % 2, position % 2


def fetch(value, dz, dy, dc):
    size = lax.axis_size("expert")
    pairs = []
    for target in range(size):
        z, y, c = locate(target)
        source = (z + dz) % (size // 4) * 4 + (y ^ dy) * 2 + (c ^ dc)
        pairs.append((source, target))
    return lax.ppermute(value, "expert", pairs)


def from_behind(shard, axis, by):
    length = lax.axis_size(axis)
    pairs = [(i, i + by) for i in range(length) if 0 <= i + by < length]
    return lax.ppermute(shard, axis, pairs)


def split_columns(gates):
    high = gates.astype(jnp.bfloat16)
    low = (gates - high.astype(jnp.float32)).astype(jnp.bfloat16)
    return high, low


def grads_kernel(count, *refs):
    blocks, (aux_ref, gate_up_ref, down_ref, out_ref) = refs[:count], refs[count:]
    width = down_ref.shape[0]
    model = gate_up_ref.shape[1]
    rows_in = jnp.concatenate([ref[0] for ref in blocks], axis=0)
    rows_grad = jnp.concatenate([ref[1] for ref in blocks], axis=0)
    contract = (((1,), (1,)), ((), ()))
    both = lax.dot_general(rows_in, gate_up_ref[...], contract, preferred_element_type=jnp.float32)
    back = lax.dot_general(rows_grad, down_ref[...], contract, preferred_element_type=jnp.float32)
    first = both[:, :width]
    second = both[:, width:]
    sigma = jax.nn.sigmoid(first)
    active = first * sigma
    aux = aux_ref[...]
    gate = aux[:, 0:1]
    slot_grad = jnp.sum(back * active * second, axis=1, keepdims=True)
    scaled = gate * back
    d_first = scaled * second * sigma * (1.0 + first * (1.0 - sigma))
    d_second = scaled * active
    d_both = jnp.concatenate([d_first, d_second], axis=1).astype(jnp.bfloat16)
    contrib = jnp.dot(d_both, gate_up_ref[...], preferred_element_type=jnp.float32)
    out_ref[:, :model] = contrib.astype(jnp.bfloat16)
    lane = lax.broadcasted_iota(jnp.int32, (aux.shape[0], PAD), 1)
    picked = jnp.where(lane % 2 == 0, aux[:, 1:2], aux[:, 2:3]) * slot_grad
    high = picked.astype(jnp.bfloat16).astype(jnp.float32)
    low = picked - high
    packed = jnp.where(lane < 2, high, jnp.where(lane < 4, low, 0.0))
    out_ref[:, model:] = packed.astype(jnp.bfloat16)


def expert_grads(blocks, aux, gate_up, down_mat):
    rows = aux.shape[0]
    model = gate_up.shape[1]
    return pl.pallas_call(
        functools.partial(grads_kernel, len(blocks)),
        out_shape=jax.ShapeDtypeStruct((rows, model + PAD), jnp.bfloat16),
        compiler_params=pltpu.CompilerParams(vmem_limit_bytes=40 << 20),
    )(*blocks, aux, gate_up, down_mat)


def unpack(block, model):
    wide = block.astype(jnp.float32)
    return wide[:, :model], wide[:, model:]


def pair_kernel(near_ref, far_ref, out_ref):
    model = out_ref.shape[1] - PAD
    total = near_ref[:, :model].astype(jnp.float32) + far_ref[:, :model].astype(jnp.float32)
    out_ref[:, :model] = total.astype(jnp.bfloat16)
    gates = near_ref[:, model:].astype(jnp.float32) + far_ref[:, model:].astype(jnp.float32)
    lane = lax.broadcasted_iota(jnp.int32, gates.shape, 1)
    shifted = pltpu.roll(gates, PAD - 2, 1)
    value = gates + shifted
    high = value.astype(jnp.bfloat16).astype(jnp.float32)
    low = pltpu.roll(value - high, 2, 1)
    packed = jnp.where(lane < 2, high, jnp.where(lane < 4, low, 0.0))
    out_ref[:, model:] = packed.astype(jnp.bfloat16)


def last_kernel(count, *refs):
    parts, (rows_ref, gates_ref) = refs[:count], refs[count:]
    model = rows_ref.shape[1]
    total = parts[0][:, :model].astype(jnp.float32)
    gates = parts[0][:, model:].astype(jnp.float32)
    for ref in parts[1:]:
        total = total + ref[:, :model].astype(jnp.float32)
        gates = gates + ref[:, model:].astype(jnp.float32)
    rows_ref[...] = total.astype(jnp.bfloat16)
    gates_ref[...] = gates + pltpu.roll(gates, PAD - 2, 1)


def body(tokens, out_grad, expert_ids, gate_weights, gate_up_rows, down_rows):
    size = lax.axis_size("expert")
    planes = size // 4
    expert_count = max(2, size // 4)
    part_count = size // expert_count
    position = lax.axis_index("expert")
    my_expert = position // part_count
    block_rows = tokens.shape[1]
    model = tokens.shape[2]
    routes = expert_ids.shape[2]
    gate_up = gate_up_rows[0, 0]
    down_mat = down_rows[0, 0]

    own = jnp.concatenate([tokens, out_grad], axis=0)
    across = [fetch(own, dz, 0, 0) for dz in range(1, planes)]
    line = [own] + across
    other = [fetch(value, 0, 1, 0) for value in line]
    near = [value for pair in zip(line, other) for value in pair]
    far = [fetch(value, 0, 0, 1) for value in near]

    half = size // 2
    z, y, c = locate(position)
    order = jnp.arange(size)
    oc, oz, oy = order // half, order % half // 2, order % 2
    source = (z + oz) % planes * 4 + (y ^ oy) * 2 + (c ^ oc)
    ids = expert_ids[0].reshape(size, block_rows, routes)[source].reshape(-1, routes)
    gates = gate_weights[0].astype(jnp.float32).reshape(size, block_rows, routes)[source].reshape(-1, routes)
    match = (ids == my_expert).astype(jnp.float32)
    gate = jnp.sum(match * gates, axis=1, keepdims=True)
    aux = jnp.concatenate([gate, match, jnp.zeros((gate.shape[0], PAD - 1 - routes), jnp.float32)], axis=1)

    rows = half * block_rows
    send = expert_grads(far, aux[rows:], gate_up, down_mat)
    keep = expert_grads(near, aux[:rows], gate_up, down_mat)
    received = fetch(send, 0, 0, 1)
    width = model + PAD
    paired = pl.pallas_call(
        pair_kernel,
        out_shape=jax.ShapeDtypeStruct((rows, width), jnp.bfloat16),
    )(keep, received).reshape(planes, 2, block_rows, width)
    parts = [paired[0, 0]]
    for dz in range(planes):
        for dy in range(2):
            if dz or dy:
                parts.append(fetch(paired[dz, dy], -dz, dy, 0))
    grad_rows, gate_lanes = pl.pallas_call(
        functools.partial(last_kernel, len(parts)),
        out_shape=(
            jax.ShapeDtypeStruct((block_rows, model), jnp.bfloat16),
            jax.ShapeDtypeStruct((block_rows, PAD), jnp.float32),
        ),
    )(*parts)
    handed = from_behind(grad_rows, "section", -1)
    return (gate_lanes[None, :, :routes], handed[None])


def solution(mesh):
    return jax.shard_map(
        body,
        mesh=mesh,
        in_specs=(
            P("section", "expert", None),
            P("section", "expert", None),
            P("section", None, None),
            P("section", None, None),
            P("section", "expert", None, None),
            P("section", "expert", None, None),
        ),
        out_specs=(P("section", "expert", None), P("section", "expert", None)),
        check_vma=False,
    )
```

time: 227 us -> 64.6 us (0.28)
  waiting for transfers between devices: 193 us -> 19.9 us
  starting transfers between devices: 1.44 us -> 24.2 us
  between operations: 13.9 us -> 0.83 us
  matrix products: 8.71 us -> 0 us
  Pallas kernels: 0 us -> 7.01 us
  local copies, waits for them, and re-layouts: 7.79 us -> 12 us
  other arithmetic: 2.49 us -> 0.17 us
    reduce_scatter x2 -> x0, waiting for transfers between devices: 116 us -> none  [the longest x1 60.5 us: body(): lax.psum_scatter(partial_value, 'expert', scatter_dimension=0, tiled=True)]
    all_gather x2 -> x0, waiting for transfers between devices: 75.3 us -> none  [the longest x1 38.2 us: body(): lax.all_gather(tokens[0], 'expert', axis=0, tiled=True)]
    ppermute x0 -> x23, starting transfers between devices: none -> 22.9 us  [fetch(): return lax.ppermute(value, 'expert', pairs)]
    ppermute x0 -> x23, waiting for transfers between devices: none -> 16.2 us  [fetch(): return lax.ppermute(value, 'expert', pairs)]
    dot_general x7 -> x0, matrix products: 8.71 us -> none  [the longest x1 3.3 us: body(): jnp.einsum('jrt,jrd->jtd', chooser, contrib.reshape(group_size, capacity,...]
    pallas_call x0 -> x4, Pallas kernels: none -> 7.01 us  [the longest x2 2.8 us: expert_grads(): pl.pallas_call(functools.partial(grads_kernel, len(blocks)), out_shape=ja...]
    ppermute x1, waiting for transfers between devices: 0.01 us -> 3.74 us  [from_behind(): return lax.ppermute(shard, axis, pairs)]
    unnamed x15 -> x26, local copies, waits for them, and re-layouts: 2.19 us -> 4.97 us
  transfers between devices with their start and end apart: 5 -> 24, of which waited for: 4 -> 10; matrix products, arithmetic and copies ran while one was open for 3% -> 7% of each run, Pallas kernels for 0% -> 2%
where the time goes in v1:
time: 64.6 us; the launch traced here: 64.1 us
  starting transfers between devices  24.2 us (37%)
  waiting for transfers between devices  19.9 us (31%)
  local copies, waits for them, and re-layouts  12 us (19%)
  Pallas kernels  7.01 us (11%)
  between operations  0.83 us (1%)
    ppermute x23, starting transfers between devices, fetch(): return lax.ppermute(value, 'expert', pairs)  22.9 us
    ppermute x23, waiting for transfers between devices, fetch(): return lax.ppermute(value, 'expert', pairs)  16.2 us
    unnamed x26, local copies, waits for them, and re-layouts  4.97 us
    ppermute x1, waiting for transfers between devices, from_behind(): return lax.ppermute(shard, axis, pairs)  3.74 us
    pallas_call x2, Pallas kernels, expert_grads(): pl.pallas_call(functools.partial(grads_kernel, len(blocks)), out_shape=ja...  2.8 us
    pallas_call x1, Pallas kernels, body(): pl.pallas_call(pair_kernel, out_shape=jax.ShapeDtypeStruct((rows, width),...  2.38 us
    pallas_call x1, Pallas kernels, body(): pl.pallas_call(functools.partial(last_kernel, len(parts)), out_shape=(jax...  1.83 us
    squeeze x1, local copies, waits for them, and re-layouts, body(): parts.append(fetch(paired[dz, dy], -dz, dy, 0))  1.78 us
  transfers between devices with their start and end apart: 24, of which 10 were waited for; matrix products, arithmetic and copies ran while one was open for 7% of the time, Pallas kernels for 2%

profile of v1, /device:TPU:0, one launch (start us, length us, event | category | flops | bytes accessed | tf_op | source)
XLA Modules:
  0.0 64.1 jit_solution(4530928063759919548)
XLA Ops:
  0.6 1.0 %constant_dynamic-update-slice_fusion.1 = bf16[2,16,2048]{2,1,0:T(8,128)(2,1)S(1)} fusion(bf16[1,16,2048]{2,1,0:T(8,128)(2,1)} %param.6), kind=kLoop, calls=%fused_computation.15 | loop fusion | bytes 131072
  1.6 0.8 %constant_dynamic-update-slice_fusion.refs_0_ = bf16[2,16,2048]{2,1,0:T(8,128)(2,1)S(1)} fusion(bf16[2,16,2048]{2,1,0:T(8,128)(2,1)S(1)} %constant_dynamic-update-slice_fusion.1, bf16[1,16,2048]{2,1,0:T(8,128)(2,1)} %param.7), kind=kLoop, calls=%fused_computation.14 | loop fusion | bytes 131072 | tf_op jit(solution)/shard_map/concatenate | solution.py:123
  2.4 3.0 %collective-permute-start = (bf16[2,16,2048]{2,1,0:T(8,128)(2,1)S(1)}, bf16[2,16,2048]{2,1,0:T(8,128)(2,1)S(1)}, u32[]{:S(2)}, u32[]{:S(2)}) collective-permute-start(bf16[2,16,2048]{2,1,0:T(8,128)(2,1)S(1)} %constant_dynamic-update-slice_fusion.refs_0_), channel_id=1, source_target_pairs={{2,0},{3,1},{0,2},{1,3},{6,4},{7,5},{4,6},{5,7},{10,8},{11,9},{8,1... | collective-permute-start | bytes 393224 | tf_op jit(solution)/shard_map/ppermute | solution.py:24
  5.4 3.6 %collective-permute-start.1 = (bf16[2,16,2048]{2,1,0:T(8,128)(2,1)S(1)}, bf16[2,16,2048]{2,1,0:T(8,128)(2,1)S(1)}, u32[]{:S(2)}, u32[]{:S(2)}) collective-permute-start(bf16[2,16,2048]{2,1,0:T(8,128)(2,1)S(1)} %constant_dynamic-update-slice_fusion.refs_0_), channel_id=1, source_target_pairs={{4,0},{5,1},{6,2},{7,3},{8,4},{9,5},{10,6},{11,7},{12,8},{13,9},{1... | collective-permute-start | bytes 393224 | tf_op jit(solution)/shard_map/ppermute | solution.py:24
  9.0 1.0 %collective-permute-start.5 = (bf16[2,16,2048]{2,1,0:T(8,128)(2,1)S(1)}, bf16[2,16,2048]{2,1,0:T(8,128)(2,1)S(1)}, u32[]{:S(2)}, u32[]{:S(2)}) collective-permute-start(bf16[2,16,2048]{2,1,0:T(8,128)(2,1)S(1)} %constant_dynamic-update-slice_fusion.refs_0_), channel_id=1, source_target_pairs={{12,0},{13,1},{14,2},{15,3},{0,4},{1,5},{2,6},{3,7},{4,8},{5,9},{6... | collective-permute-start | bytes 393224 | tf_op jit(solution)/shard_map/ppermute | solution.py:24
  10.0 0.8 %reshape_squeeze.3 = s32[16,16,2]{1,0,2:T(8,128)S(1)} reshape(s32[1,256,2]{1,2,0:T(2,128)} %param.8) | data formatting | bytes 4096 | tf_op jit(solution)/shard_map/reshape;squeeze | solution.py:135
  10.9 0.6 gather_fusion
  11.6 0.8 %reshape.198 = f32[16,16,2]{1,0,2:T(8,128)S(1)} reshape(bf16[1,256,2]{1,2,0:T(2,128)(2,1)} %param.9) | data formatting | bytes 3072 | tf_op jit(solution)/shard_map/convert_element_type | solution.py:136
  12.4 0.6 gather_fusion.1
  14.0 5.8 %collective-permute-done.3.refs_4_ = bf16[2,16,2048]{2,1,0:T(8,128)(2,1)S(1)} collective-permute-done((bf16[2,16,2048]{2,1,0:T(8,128)(2,1)S(1)}, bf16[2,16,2048]{2,1,0:T(8,128)(2,1)S(1)}, u32[]{:S(2)}, u32[]{:S(2)}) %collective-permute-start.3) | collective-permute-done | bytes 131104 | tf_op jit(solution)/shard_map/ppermute | solution.py:24
  20.3 1.5 %collective-permute-start.6 = (bf16[2,16,2048]{2,1,0:T(8,128)(2,1)S(1)}, bf16[2,16,2048]{2,1,0:T(8,128)(2,1)S(1)}, u32[]{:S(2)}, u32[]{:S(2)}) collective-permute-start(bf16[2,16,2048]{2,1,0:T(8,128)(2,1)S(1)} %collective-permute-done.5.refs_6_), channel_id=1, source_target_pairs={{2,0},{3,1},{0,2},{1,3},{6,4},{7,5},{4,6},{5,7},{10,8},{11,9},{8,1... | collective-permute-start | bytes 393224 | tf_op jit(solution)/shard_map/ppermute | solution.py:24
  22.5 3.3 %collective-permute-done.4.refs_5_ = bf16[2,16,2048]{2,1,0:T(8,128)(2,1)S(1)} collective-permute-done((bf16[2,16,2048]{2,1,0:T(8,128)(2,1)S(1)}, bf16[2,16,2048]{2,1,0:T(8,128)(2,1)S(1)}, u32[]{:S(2)}, u32[]{:S(2)}) %collective-permute-start.4) | collective-permute-done | bytes 131104 | tf_op jit(solution)/shard_map/ppermute | solution.py:24
  25.9 1.4 %collective-permute-done.6.refs_7_ = bf16[2,16,2048]{2,1,0:T(8,128)(2,1)S(1)} collective-permute-done((bf16[2,16,2048]{2,1,0:T(8,128)(2,1)S(1)}, bf16[2,16,2048]{2,1,0:T(8,128)(2,1)S(1)}, u32[]{:S(2)}, u32[]{:S(2)}) %collective-permute-start.6) | collective-permute-done | bytes 131104 | tf_op jit(solution)/shard_map/ppermute | solution.py:24
  27.9 0.7 %collective-permute-done.10.refs_3_ = bf16[2,16,2048]{2,1,0:T(8,128)(2,1)S(1)} collective-permute-done((bf16[2,16,2048]{2,1,0:T(8,128)(2,1)S(1)}, bf16[2,16,2048]{2,1,0:T(8,128)(2,1)S(1)}, u32[]{:S(2)}, u32[]{:S(2)}) %collective-permute-start.10) | collective-permute-done | bytes 131104 | tf_op jit(solution)/shard_map/ppermute | solution.py:24
  29.1 1.1 %copy-done.1 = bf16[1,1,192,2048]{3,2,1,0:T(8,128)(2,1)S(1)} copy-done((bf16[1,1,192,2048]{3,2,1,0:T(8,128)(2,1)S(1)}, bf16[1,1,192,2048]{3,2,1,0:T(8,128)(2,1)}, u32[]{:S(2)}) %copy-start.1) | copy-done | bytes 786456
  30.3 1.4 %shard_map.78 = bf16[128,2176]{1,0:T(8,128)(2,1)S(1)} custom-call(bf16[2,16,2048]{2,1,0:T(8,128)(2,1)S(1)} %collective-permute-done.7.refs_0_, bf16[2,16,2048]{2,1,0:T(8,128)(2,1)S(1)} %collective-permute-done.8.refs_1_, bf16[2,16,2048]{2,1,0:T(8,128)(2,1)S(1)} %collective-permute-done.9.refs_2_, bf16[2,16,2048]{2,1,0:T(8,128)(2,1)S(1)} %collective-permute-done.10.refs_3_, ...), custom_call_target="tpu_custom_call" | custom-call | tf_op jit(solution)/shard_map/pallas_call | solution.py:72
  31.9 1.4 %shard_map.77.near_ref = bf16[128,2176]{1,0:T(8,128)(2,1)S(1)} custom-call(bf16[2,16,2048]{2,1,0:T(8,128)(2,1)S(1)} %constant_dynamic-update-slice_fusion.refs_0_, bf16[2,16,2048]{2,1,0:T(8,128)(2,1)S(1)} %collective-permute-done.refs_1_, bf16[2,16,2048]{2,1,0:T(8,128)(2,1)S(1)} %collective-permute-done.1.refs_2_, ...), custom_call_target="tpu_custom_call" | custom-call | tf_op jit(solution)/shard_map/pallas_call | solution.py:72
  33.4 0.8 %copy-done.3 = bf16[128,2176]{1,0:T(8,128)(2,1)} copy-done((bf16[128,2176]{1,0:T(8,128)(2,1)}, bf16[128,2176]{1,0:T(8,128)(2,1)S(1)}, u32[]{:S(2)}) %copy-start.3) | copy-done | bytes 557080
  34.2 0.8 %copy-done.4 = bf16[128,2176]{1,0:T(8,128)(2,1)} copy-done((bf16[128,2176]{1,0:T(8,128)(2,1)}, bf16[128,2176]{1,0:T(8,128)(2,1)S(1)}, u32[]{:S(2)}) %copy-start.4) | copy-done | bytes 557080
  35.0 2.4 %shard_map.79 = bf16[128,2176]{1,0:T(8,128)(2,1)} custom-call(bf16[128,2176]{1,0:T(8,128)(2,1)} %copy-done.3, bf16[128,2176]{1,0:T(8,128)(2,1)} %copy-done.4), custom_call_target="tpu_custom_call" | custom-call | tf_op jit(solution)/shard_map/pallas_call | solution.py:146
  37.4 1.8 %slice_bitcast_fusion = (bf16[16,2176]{1,0:T(8,128)(2,1)S(1)}, bf16[16,2176]{1,0:T(8,128)(2,1)S(1)}, bf16[16,2176]{1,0:T(8,128)(2,1)S(1)}, bf16[16,2176]{1,0:T(8...) fusion(bf16[4,2,16,2176]{3,2,1,0:T(8,128)(2,1)} %bitcast.33), kind=kLoop, calls=%fused_computation.3 | loop fusion | bytes 1114112 | tf_op jit(solution)/shard_map/squeeze | solution.py:154
  39.7 1.8 %collective-permute-start.18 = (bf16[16,2176]{1,0:T(8,128)(2,1)S(1)}, bf16[16,2176]{1,0:T(8,128)(2,1)S(1)}, u32[]{:S(2)}, u32[]{:S(2)}) collective-permute-start(bf16[16,2176]{1,0:T(8,128)(2,1)S(1)} %get-tuple-element.10), channel_id=1, source_target_pairs={{14,0},{15,1},{12,2},{13,3},{2,4},{3,5},{0,6},{1,7},{6,8},{7,9},{4... | collective-permute-start | bytes 208904 | tf_op jit(solution)/shard_map/ppermute | solution.py:24
  41.4 3.6 %collective-permute-start.19 = (bf16[16,2176]{1,0:T(8,128)(2,1)S(1)}, bf16[16,2176]{1,0:T(8,128)(2,1)S(1)}, u32[]{:S(2)}, u32[]{:S(2)}) collective-permute-start(bf16[16,2176]{1,0:T(8,128)(2,1)S(1)} %get-tuple-element.9), channel_id=1, source_target_pairs={{8,0},{9,1},{10,2},{11,3},{12,4},{13,5},{14,6},{15,7},{0,8},{1,9},... | collective-permute-start | bytes 208904 | tf_op jit(solution)/shard_map/ppermute | solution.py:24
  45.0 2.4 %collective-permute-start.21 = (bf16[16,2176]{1,0:T(8,128)(2,1)S(1)}, bf16[16,2176]{1,0:T(8,128)(2,1)S(1)}, u32[]{:S(2)}, u32[]{:S(2)}) collective-permute-start(bf16[16,2176]{1,0:T(8,128)(2,1)S(1)} %get-tuple-element.7), channel_id=1, source_target_pairs={{4,0},{5,1},{6,2},{7,3},{8,4},{9,5},{10,6},{11,7},{12,8},{13,9},{1... | collective-permute-start | bytes 208904 | tf_op jit(solution)/shard_map/ppermute | solution.py:24
  47.4 2.9 %collective-permute-start.22 = (bf16[16,2176]{1,0:T(8,128)(2,1)S(1)}, bf16[16,2176]{1,0:T(8,128)(2,1)S(1)}, u32[]{:S(2)}, u32[]{:S(2)}) collective-permute-start(bf16[16,2176]{1,0:T(8,128)(2,1)S(1)} %get-tuple-element.6), channel_id=1, source_target_pairs={{6,0},{7,1},{4,2},{5,3},{10,4},{11,5},{8,6},{9,7},{14,8},{15,9},{1... | collective-permute-start | bytes 208904 | tf_op jit(solution)/shard_map/ppermute | solution.py:24
  50.3 1.6 %collective-permute-done.19.refs_4_ = bf16[16,2176]{1,0:T(8,128)(2,1)S(1)} collective-permute-done((bf16[16,2176]{1,0:T(8,128)(2,1)S(1)}, bf16[16,2176]{1,0:T(8,128)(2,1)S(1)}, u32[]{:S(2)}, u32[]{:S(2)}) %collective-permute-start.19) | collective-permute-done | bytes 69664 | tf_op jit(solution)/shard_map/ppermute | solution.py:24
  51.9 2.2 %collective-permute-done.20.refs_5_ = bf16[16,2176]{1,0:T(8,128)(2,1)S(1)} collective-permute-done((bf16[16,2176]{1,0:T(8,128)(2,1)S(1)}, bf16[16,2176]{1,0:T(8,128)(2,1)S(1)}, u32[]{:S(2)}, u32[]{:S(2)}) %collective-permute-start.20) | collective-permute-done | bytes 69664 | tf_op jit(solution)/shard_map/ppermute | solution.py:24
  55.3 1.8 %shard_map.80 = (bf16[16,2048]{1,0:T(8,128)(2,1)}, f32[16,128]{1,0:T(8,128)}) custom-call(bf16[16,2176]{1,0:T(8,128)(2,1)} %get-tuple-element.13.refs_0_, bf16[16,2176]{1,0:T(8,128)(2,1)} %copy-done.5, bf16[16,2176]{1,0:T(8,128)(2,1)} %copy-done.6, bf16[16,2176]{1,0:T(8,128)(2,1)} %copy-done.7, bf16[16,2176]{1,0:T(8,128)(2,1)} %copy-done.8, ...), custom_call_target="tpu_custom_call" | custom-call | tf_op jit(solution)/shard_map/pallas_call | solution.py:155
  57.1 1.3 %collective-permute-start.23 = (bf16[16,2048]{1,0:T(8,128)(2,1)}, bf16[16,2048]{1,0:T(8,128)(2,1)S(1)}, u32[]{:S(2)}, u32[]{:S(2)}) collective-permute-start(bf16[16,2048]{1,0:T(8,128)(2,1)} %get-tuple-element.5), channel_id=1, source_target_pairs={{16,0},{17,1},{18,2},{19,3},{20,4},{21,5},{22,6},{23,7},{24,8},{25... | collective-permute-start | bytes 196616 | tf_op jit(solution)/shard_map/ppermute | solution.py:30
  58.4 1.3 %copy.16 = f32[16,2]{0,1:T(2,128)} copy(f32[16,2]{1,0:T(8,128)} %bitcast.36) | data formatting | bytes 256 | tf_op jit(solution)/shard_map/slice | solution.py:163
  59.8 3.7 %collective-permute-done.23 = bf16[16,2048]{1,0:T(8,128)(2,1)S(1)} collective-permute-done((bf16[16,2048]{1,0:T(8,128)(2,1)}, bf16[16,2048]{1,0:T(8,128)(2,1)S(1)}, u32[]{:S(2)}, u32[]{:S(2)}) %collective-permute-start.23) | collective-permute-done | bytes 65568 | tf_op jit(solution)/shard_map/ppermute | solution.py:30
  63.5 0.6 copy.19
  (65 shorter events, 5.4 us)
Async XLA Ops:
  0.6 28.5 %copy-start = (bf16[1,1,384,2048]{3,2,1,0:T(8,128)(2,1)S(1)}, bf16[1,1,384,2048]{3,2,1,0:T(8,128)(2,1)}, u32[]{:S(2)}) copy-start(bf16[1,1,384,2048]{3,2,1,0:T(8,128)(2,1)} %param.10) | copy-start | bytes 4718596
  2.4 11.3 %collective-permute-start = (bf16[2,16,2048]{2,1,0:T(8,128)(2,1)S(1)}, bf16[2,16,2048]{2,1,0:T(8,128)(2,1)S(1)}, u32[]{:S(2)}, u32[]{:S(2)}) collective-permute-start(bf16[2,16,2048]{2,1,0:T(8,128)(2,1)S(1)} %constant_dynamic-update-slice_fusion.refs_0_), channel_id=1, source_target_pairs={{2,0},{3,1},{0,2},{1,3},{6,4},{7,5},{4,6},{5,7},{10,8},{11,9},{8,1... | collective-permute-start | bytes 393224 | tf_op jit(solution)/shard_map/ppermute | solution.py:24
  5.4 7.8 %collective-permute-start.1 = (bf16[2,16,2048]{2,1,0:T(8,128)(2,1)S(1)}, bf16[2,16,2048]{2,1,0:T(8,128)(2,1)S(1)}, u32[]{:S(2)}, u32[]{:S(2)}) collective-permute-start(bf16[2,16,2048]{2,1,0:T(8,128)(2,1)S(1)} %constant_dynamic-update-slice_fusion.refs_0_), channel_id=1, source_target_pairs={{4,0},{5,1},{6,2},{7,3},{8,4},{9,5},{10,6},{11,7},{12,8},{13,9},{1... | collective-permute-start | bytes 393224 | tf_op jit(solution)/shard_map/ppermute | solution.py:24
  9.0 10.8 %collective-permute-start.3 = (bf16[2,16,2048]{2,1,0:T(8,128)(2,1)S(1)}, bf16[2,16,2048]{2,1,0:T(8,128)(2,1)S(1)}, u32[]{:S(2)}, u32[]{:S(2)}) collective-permute-start(bf16[2,16,2048]{2,1,0:T(8,128)(2,1)S(1)} %constant_dynamic-update-slice_fusion.refs_0_), channel_id=1, source_target_pairs={{8,0},{9,1},{10,2},{11,3},{12,4},{13,5},{14,6},{15,7},{0,8},{1,9},... | collective-permute-start | bytes 393224 | tf_op jit(solution)/shard_map/ppermute | solution.py:24
  9.0 11.3 %collective-permute-start.5 = (bf16[2,16,2048]{2,1,0:T(8,128)(2,1)S(1)}, bf16[2,16,2048]{2,1,0:T(8,128)(2,1)S(1)}, u32[]{:S(2)}, u32[]{:S(2)}) collective-permute-start(bf16[2,16,2048]{2,1,0:T(8,128)(2,1)S(1)} %constant_dynamic-update-slice_fusion.refs_0_), channel_id=1, source_target_pairs={{12,0},{13,1},{14,2},{15,3},{0,4},{1,5},{2,6},{3,7},{4,8},{5,9},{6... | collective-permute-start | bytes 393224 | tf_op jit(solution)/shard_map/ppermute | solution.py:24
  10.0 11.8 %collective-permute-start.7 = (bf16[2,16,2048]{2,1,0:T(8,128)(2,1)S(1)}, bf16[2,16,2048]{2,1,0:T(8,128)(2,1)S(1)}, u32[]{:S(2)}, u32[]{:S(2)}) collective-permute-start(bf16[2,16,2048]{2,1,0:T(8,128)(2,1)S(1)} %constant_dynamic-update-slice_fusion.refs_0_), channel_id=1, source_target_pairs={{1,0},{0,1},{3,2},{2,3},{5,4},{4,5},{7,6},{6,7},{9,8},{8,9},{11,10... | collective-permute-start | bytes 393224 | tf_op jit(solution)/shard_map/ppermute | solution.py:24
  13.2 8.7 %collective-permute-start.2 = (bf16[2,16,2048]{2,1,0:T(8,128)(2,1)S(1)}, bf16[2,16,2048]{2,1,0:T(8,128)(2,1)S(1)}, u32[]{:S(2)}, u32[]{:S(2)}) collective-permute-start(bf16[2,16,2048]{2,1,0:T(8,128)(2,1)S(1)} %collective-permute-done.1.refs_2_), channel_id=1, source_target_pairs={{2,0},{3,1},{0,2},{1,3},{6,4},{7,5},{4,6},{5,7},{10,8},{11,9},{8,1... | collective-permute-start | bytes 393224 | tf_op jit(solution)/shard_map/ppermute | solution.py:24
  13.8 14.0 %collective-permute-start.9 = (bf16[2,16,2048]{2,1,0:T(8,128)(2,1)S(1)}, bf16[2,16,2048]{2,1,0:T(8,128)(2,1)S(1)}, u32[]{:S(2)}, u32[]{:S(2)}) collective-permute-start(bf16[2,16,2048]{2,1,0:T(8,128)(2,1)S(1)} %collective-permute-done.1.refs_2_), channel_id=1, source_target_pairs={{1,0},{0,1},{3,2},{2,3},{5,4},{4,5},{7,6},{6,7},{9,8},{8,9},{11,10... | collective-permute-start | bytes 393224 | tf_op jit(solution)/shard_map/ppermute | solution.py:24
  19.8 6.0 %collective-permute-start.4 = (bf16[2,16,2048]{2,1,0:T(8,128)(2,1)S(1)}, bf16[2,16,2048]{2,1,0:T(8,128)(2,1)S(1)}, u32[]{:S(2)}, u32[]{:S(2)}) collective-permute-start(bf16[2,16,2048]{2,1,0:T(8,128)(2,1)S(1)} %collective-permute-done.3.refs_4_), channel_id=1, source_target_pairs={{2,0},{3,1},{0,2},{1,3},{6,4},{7,5},{4,6},{5,7},{10,8},{11,9},{8,1... | collective-permute-start | bytes 393224 | tf_op jit(solution)/shard_map/ppermute | solution.py:24
  20.3 6.9 %collective-permute-start.6 = (bf16[2,16,2048]{2,1,0:T(8,128)(2,1)S(1)}, bf16[2,16,2048]{2,1,0:T(8,128)(2,1)S(1)}, u32[]{:S(2)}, u32[]{:S(2)}) collective-permute-start(bf16[2,16,2048]{2,1,0:T(8,128)(2,1)S(1)} %collective-permute-done.5.refs_6_), channel_id=1, source_target_pairs={{2,0},{3,1},{0,2},{1,3},{6,4},{7,5},{4,6},{5,7},{10,8},{11,9},{8,1... | collective-permute-start | bytes 393224 | tf_op jit(solution)/shard_map/ppermute | solution.py:24
  21.9 5.4 %collective-permute-start.8 = (bf16[2,16,2048]{2,1,0:T(8,128)(2,1)S(1)}, bf16[2,16,2048]{2,1,0:T(8,128)(2,1)S(1)}, u32[]{:S(2)}, u32[]{:S(2)}) collective-permute-start(bf16[2,16,2048]{2,1,0:T(8,128)(2,1)S(1)} %collective-permute-done.refs_1_), channel_id=1, source_target_pairs={{1,0},{0,1},{3,2},{2,3},{5,4},{4,5},{7,6},{6,7},{9,8},{8,9},{11,10... | collective-permute-start | bytes 393224 | tf_op jit(solution)/shard_map/ppermute | solution.py:24
  22.0 5.9 %collective-permute-start.11 = (bf16[2,16,2048]{2,1,0:T(8,128)(2,1)S(1)}, bf16[2,16,2048]{2,1,0:T(8,128)(2,1)S(1)}, u32[]{:S(2)}, u32[]{:S(2)}) collective-permute-start(bf16[2,16,2048]{2,1,0:T(8,128)(2,1)S(1)} %collective-permute-done.3.refs_4_), channel_id=1, source_target_pairs={{1,0},{0,1},{3,2},{2,3},{5,4},{4,5},{7,6},{6,7},{9,8},{8,9},{11,10... | collective-permute-start | bytes 393224 | tf_op jit(solution)/shard_map/ppermute | solution.py:24
  25.9 2.0 %collective-permute-start.13 = (bf16[2,16,2048]{2,1,0:T(8,128)(2,1)S(1)}, bf16[2,16,2048]{2,1,0:T(8,128)(2,1)S(1)}, u32[]{:S(2)}, u32[]{:S(2)}) collective-permute-start(bf16[2,16,2048]{2,1,0:T(8,128)(2,1)S(1)} %collective-permute-done.5.refs_6_), channel_id=1, source_target_pairs={{1,0},{0,1},{3,2},{2,3},{5,4},{4,5},{7,6},{6,7},{9,8},{8,9},{11,10... | collective-permute-start | bytes 393224 | tf_op jit(solution)/shard_map/ppermute | solution.py:24
  27.3 1.3 %collective-permute-start.10 = (bf16[2,16,2048]{2,1,0:T(8,128)(2,1)S(1)}, bf16[2,16,2048]{2,1,0:T(8,128)(2,1)S(1)}, u32[]{:S(2)}, u32[]{:S(2)}) collective-permute-start(bf16[2,16,2048]{2,1,0:T(8,128)(2,1)S(1)} %collective-permute-done.2.refs_3_), channel_id=1, source_target_pairs={{1,0},{0,1},{3,2},{2,3},{5,4},{4,5},{7,6},{6,7},{9,8},{8,9},{11,10... | collective-permute-start | bytes 393224 | tf_op jit(solution)/shard_map/ppermute | solution.py:24
  27.3 1.5 %collective-permute-start.12 = (bf16[2,16,2048]{2,1,0:T(8,128)(2,1)S(1)}, bf16[2,16,2048]{2,1,0:T(8,128)(2,1)S(1)}, u32[]{:S(2)}, u32[]{:S(2)}) collective-permute-start(bf16[2,16,2048]{2,1,0:T(8,128)(2,1)S(1)} %collective-permute-done.4.refs_5_), channel_id=1, source_target_pairs={{1,0},{0,1},{3,2},{2,3},{5,4},{4,5},{7,6},{6,7},{9,8},{8,9},{11,10... | collective-permute-start | bytes 393224 | tf_op jit(solution)/shard_map/ppermute | solution.py:24
  27.8 1.3 %collective-permute-start.14 = (bf16[2,16,2048]{2,1,0:T(8,128)(2,1)S(1)}, bf16[2,16,2048]{2,1,0:T(8,128)(2,1)S(1)}, u32[]{:S(2)}, u32[]{:S(2)}) collective-permute-start(bf16[2,16,2048]{2,1,0:T(8,128)(2,1)S(1)} %collective-permute-done.6.refs_7_), channel_id=1, source_target_pairs={{1,0},{0,1},{3,2},{2,3},{5,4},{4,5},{7,6},{6,7},{9,8},{8,9},{11,10... | collective-permute-start | bytes 393224 | tf_op jit(solution)/shard_map/ppermute | solution.py:24
  29.1 1.1 %copy-start.1 = (bf16[1,1,192,2048]{3,2,1,0:T(8,128)(2,1)S(1)}, bf16[1,1,192,2048]{3,2,1,0:T(8,128)(2,1)}, u32[]{:S(2)}) copy-start(bf16[1,1,192,2048]{3,2,1,0:T(8,128)(2,1)} %param.11) | copy-start | bytes 2359300
  30.3 1.7 %copy-start.2 = (bf16[1,1,192,2048]{3,2,1,0:T(8,128)(2,1)S(1)}, bf16[1,1,192,2048]{3,2,1,0:T(8,128)(2,1)}, u32[]{:S(2)}) copy-start(bf16[1,1,192,2048]{3,2,1,0:T(8,128)(2,1)} %param.11) | copy-start | bytes 2359300
  31.7 2.5 %collective-permute-start.15 = (bf16[128,2176]{1,0:T(8,128)(2,1)S(1)}, bf16[128,2176]{1,0:T(8,128)(2,1)S(1)}, u32[]{:S(2)}, u32[]{:S(2)}) collective-permute-start(bf16[128,2176]{1,0:T(8,128)(2,1)S(1)} %shard_map.78), channel_id=1, source_target_pairs={{1,0},{0,1},{3,2},{2,3},{5,4},{4,5},{7,6},{6,7},{9,8},{8,9},{11,10... | collective-permute-start | bytes 1671176 | tf_op jit(solution)/shard_map/ppermute | solution.py:24
  33.4 0.8 %copy-start.3 = (bf16[128,2176]{1,0:T(8,128)(2,1)}, bf16[128,2176]{1,0:T(8,128)(2,1)S(1)}, u32[]{:S(2)}) copy-start(bf16[128,2176]{1,0:T(8,128)(2,1)S(1)} %shard_map.77.near_ref) | copy-start | bytes 1671172
  39.1 5.9 %collective-permute-start.16 = (bf16[16,2176]{1,0:T(8,128)(2,1)S(1)}, bf16[16,2176]{1,0:T(8,128)(2,1)S(1)}, u32[]{:S(2)}, u32[]{:S(2)}) collective-permute-start(bf16[16,2176]{1,0:T(8,128)(2,1)S(1)} %get-tuple-element.12), channel_id=1, source_target_pairs={{2,0},{3,1},{0,2},{1,3},{6,4},{7,5},{4,6},{5,7},{10,8},{11,9},{8,1... | collective-permute-start | bytes 208904 | tf_op jit(solution)/shard_map/ppermute | solution.py:24
  39.6 7.7 %collective-permute-start.17 = (bf16[16,2176]{1,0:T(8,128)(2,1)S(1)}, bf16[16,2176]{1,0:T(8,128)(2,1)S(1)}, u32[]{:S(2)}, u32[]{:S(2)}) collective-permute-start(bf16[16,2176]{1,0:T(8,128)(2,1)S(1)} %get-tuple-element.11), channel_id=1, source_target_pairs={{12,0},{13,1},{14,2},{15,3},{0,4},{1,5},{2,6},{3,7},{4,8},{5,9},{6... | collective-permute-start | bytes 208904 | tf_op jit(solution)/shard_map/ppermute | solution.py:24
  39.7 10.7 %collective-permute-start.18 = (bf16[16,2176]{1,0:T(8,128)(2,1)S(1)}, bf16[16,2176]{1,0:T(8,128)(2,1)S(1)}, u32[]{:S(2)}, u32[]{:S(2)}) collective-permute-start(bf16[16,2176]{1,0:T(8,128)(2,1)S(1)} %get-tuple-element.10), channel_id=1, source_target_pairs={{14,0},{15,1},{12,2},{13,3},{2,4},{3,5},{0,6},{1,7},{6,8},{7,9},{4... | collective-permute-start | bytes 208904 | tf_op jit(solution)/shard_map/ppermute | solution.py:24
  41.4 10.5 %collective-permute-start.19 = (bf16[16,2176]{1,0:T(8,128)(2,1)S(1)}, bf16[16,2176]{1,0:T(8,128)(2,1)S(1)}, u32[]{:S(2)}, u32[]{:S(2)}) collective-permute-start(bf16[16,2176]{1,0:T(8,128)(2,1)S(1)} %get-tuple-element.9), channel_id=1, source_target_pairs={{8,0},{9,1},{10,2},{11,3},{12,4},{13,5},{14,6},{15,7},{0,8},{1,9},... | collective-permute-start | bytes 208904 | tf_op jit(solution)/shard_map/ppermute | solution.py:24
  45.0 9.1 %collective-permute-start.20 = (bf16[16,2176]{1,0:T(8,128)(2,1)S(1)}, bf16[16,2176]{1,0:T(8,128)(2,1)S(1)}, u32[]{:S(2)}, u32[]{:S(2)}) collective-permute-start(bf16[16,2176]{1,0:T(8,128)(2,1)S(1)} %get-tuple-element.8), channel_id=1, source_target_pairs={{10,0},{11,1},{8,2},{9,3},{14,4},{15,5},{12,6},{13,7},{2,8},{3,9},... | collective-permute-start | bytes 208904 | tf_op jit(solution)/shard_map/ppermute | solution.py:24
  45.0 9.7 %copy-start.5 = (bf16[16,2176]{1,0:T(8,128)(2,1)}, bf16[16,2176]{1,0:T(8,128)(2,1)S(1)}, u32[]{:S(2)}) copy-start(bf16[16,2176]{1,0:T(8,128)(2,1)S(1)} %collective-permute-done.16.refs_1_) | copy-start | bytes 208900
  45.0 9.1 %collective-permute-start.21 = (bf16[16,2176]{1,0:T(8,128)(2,1)S(1)}, bf16[16,2176]{1,0:T(8,128)(2,1)S(1)}, u32[]{:S(2)}, u32[]{:S(2)}) collective-permute-start(bf16[16,2176]{1,0:T(8,128)(2,1)S(1)} %get-tuple-element.7), channel_id=1, source_target_pairs={{4,0},{5,1},{6,2},{7,3},{8,4},{9,5},{10,6},{11,7},{12,8},{13,9},{1... | collective-permute-start | bytes 208904 | tf_op jit(solution)/shard_map/ppermute | solution.py:24
  47.4 7.3 %copy-start.6 = (bf16[16,2176]{1,0:T(8,128)(2,1)}, bf16[16,2176]{1,0:T(8,128)(2,1)S(1)}, u32[]{:S(2)}) copy-start(bf16[16,2176]{1,0:T(8,128)(2,1)S(1)} %collective-permute-done.17.refs_2_) | copy-start | bytes 208900
  47.4 7.3 %collective-permute-start.22 = (bf16[16,2176]{1,0:T(8,128)(2,1)S(1)}, bf16[16,2176]{1,0:T(8,128)(2,1)S(1)}, u32[]{:S(2)}, u32[]{:S(2)}) collective-permute-start(bf16[16,2176]{1,0:T(8,128)(2,1)S(1)} %get-tuple-element.6), channel_id=1, source_target_pairs={{6,0},{7,1},{4,2},{5,3},{10,4},{11,5},{8,6},{9,7},{14,8},{15,9},{1... | collective-permute-start | bytes 208904 | tf_op jit(solution)/shard_map/ppermute | solution.py:24
  50.3 4.4 %copy-start.7 = (bf16[16,2176]{1,0:T(8,128)(2,1)}, bf16[16,2176]{1,0:T(8,128)(2,1)S(1)}, u32[]{:S(2)}) copy-start(bf16[16,2176]{1,0:T(8,128)(2,1)S(1)} %collective-permute-done.18.refs_3_) | copy-start | bytes 208900
  51.9 2.8 %copy-start.8 = (bf16[16,2176]{1,0:T(8,128)(2,1)}, bf16[16,2176]{1,0:T(8,128)(2,1)S(1)}, u32[]{:S(2)}) copy-start(bf16[16,2176]{1,0:T(8,128)(2,1)S(1)} %collective-permute-done.19.refs_4_) | copy-start | bytes 208900
  57.1 6.4 %collective-permute-start.23 = (bf16[16,2048]{1,0:T(8,128)(2,1)}, bf16[16,2048]{1,0:T(8,128)(2,1)S(1)}, u32[]{:S(2)}, u32[]{:S(2)}) collective-permute-start(bf16[16,2048]{1,0:T(8,128)(2,1)} %get-tuple-element.5), channel_id=1, source_target_pairs={{16,0},{17,1},{18,2},{19,3},{20,4},{21,5},{22,6},{23,7},{24,8},{25... | collective-permute-start | bytes 196616 | tf_op jit(solution)/shard_map/ppermute | solution.py:30
  (4 other events, 2.7 us)

commit v2 on v0

v2 whole, which is shorter than its diff:
```python
import functools

import jax
import jax.numpy as jnp
from jax import lax
from jax.experimental import pallas as pl
from jax.experimental.pallas import tpu as pltpu
from jax.sharding import PartitionSpec as P

PAD = 128


def slot_offsets(planes):
    half = planes // 2
    far = [(half + k, 0) for k in range(half)]
    near = [(k + 1, 0) for k in range(half - 1)] + [(0, 1)]
    slots = list(zip(far, near))
    return slots + [((a[0], 1), (b[0], 1 - b[1])) for a, b in slots]


def exchange(value, ahead, behind):
    pairs = []
    for here in range(lax.axis_size("expert")):
        z, y, c = here // 4, here // 2 % 2, here % 2
        dz, dy = ahead if c else behind
        pairs.append((here, (z ^ dz) * 4 + (y ^ dy) * 2 + c))
    return lax.ppermute(value, "expert", pairs)


def swap(value):
    return lax.ppermute(value, "expert", [(i, i ^ 1) for i in range(lax.axis_size("expert"))])


def from_behind(shard, axis, by):
    length = lax.axis_size(axis)
    pairs = [(i, i + by) for i in range(length) if 0 <= i + by < length]
    return lax.ppermute(shard, axis, pairs)


def after(value, *others):
    return lax.optimization_barrier((value,) + others)[0]


def in_hbm(value):
    return pltpu.with_memory_space_constraint(value, pltpu.HBM)


def pack_kernel(a_ref, b_ref, c_ref, d_ref, out_ref, sems):
    copies = [
        pltpu.make_async_copy(ref, out_ref.at[i], sems.at[i]) for i, ref in enumerate((a_ref, b_ref, c_ref, d_ref))
    ]
    for copy in copies:
        copy.start()
    for copy in copies:
        copy.wait()


def stage_kernel(planes, rows, ids_ref, gates_ref, up_ref, down_ref, _, out_ref, up_out, down_out, gate_ref, sems):
    copies = [
        pltpu.make_async_copy(up_ref, up_out, sems.at[0]),
        pltpu.make_async_copy(down_ref, down_out, sems.at[1]),
    ]
    for copy in copies:
        copy.start()
    position = lax.axis_index("expert")
    z, y, c = position // 4, position // 2 % 2, position % 2
    expert = position // (4 * planes // max(2, planes))
    match = (ids_ref[...] == expert).astype(jnp.float32)
    gate = jnp.sum(match * gates_ref[...].astype(jnp.float32), axis=0, keepdims=True)
    table = jnp.concatenate([gate, match, jnp.zeros((8 - 1 - match.shape[0], gate.shape[1]), jnp.float32)], axis=0)
    columns = jnp.transpose(table)
    gate_ref[...] = columns.reshape(gate_ref.shape)
    at = 0
    slots = slot_offsets(planes)
    for core in (c, c ^ 1):
        for ahead, behind in slots:
            dz = jnp.where(core == 1, ahead[0], behind[0])
            dy = jnp.where(core == 1, ahead[1], behind[1])
            chip = (z ^ dz) * 2 + (y ^ dy)
            for unit in (0, 1):
                out_ref[at:at + rows] = gate_ref[chip * 2 + (core ^ unit)]
                at += rows
    for copy in copies:
        copy.wait()


def grads_kernel(near, *refs):
    blocks, (chip_ref, aux_ref, gate_up_ref, down_ref, out_ref) = refs[:-5], refs[-5:]
    width = down_ref.shape[0]
    model = gate_up_ref.shape[1]
    units = [[ref[i] for i in range(4)] for ref in blocks]
    odd_core = lax.axis_index("expert") % 2 == 1
    chip = [chip_ref[i] for i in range(4)]
    if near:
        units[-1] = [jnp.where(odd_core, a, b) for a, b in zip(units[-1], chip)]
    else:
        units[-1] = [jnp.where(odd_core, b, a) for a, b in zip(units[-1], chip[2:] + chip[:2])]
    rows_in = jnp.concatenate([unit[i] for unit in units for i in (0, 2)], axis=0)
    rows_grad = jnp.concatenate([unit[i] for unit in units for i in (1, 3)], axis=0)
    contract = (((1,), (1,)), ((), ()))
    both = lax.dot_general(rows_in, gate_up_ref[...], contract, preferred_element_type=jnp.float32)
    back = lax.dot_general(rows_grad, down_ref[...], contract, preferred_element_type=jnp.float32)
    first = both[:, :width]
    second = both[:, width:]
    sigma = jax.nn.sigmoid(first)
    active = first * sigma
    gate = aux_ref[:, 0:1]
    slot_grad = jnp.sum(back * active * second, axis=1, keepdims=True)
    scaled = gate * back
    d_first = scaled * second * sigma * (1.0 + first * (1.0 - sigma))
    d_second = scaled * active
    d_both = jnp.concatenate([d_first, d_second], axis=1).astype(jnp.bfloat16)
    contrib = jnp.dot(d_both, gate_up_ref[...], preferred_element_type=jnp.float32)
    out_ref[:, :model] = contrib.astype(out_ref.dtype)
    lane = lax.broadcasted_iota(jnp.int32, (slot_grad.shape[0], PAD), 1)
    picked = jnp.where(lane % 2 == 0, aux_ref[:, 1:2], aux_ref[:, 2:3]) * slot_grad
    high = picked.astype(jnp.bfloat16).astype(jnp.float32)
    place = lane - (0 if near else 4)
    packed = jnp.where(place // 2 == 0, high, jnp.where(place // 2 == 1, picked - high, 0.0))
    out_ref[:, model:] = packed.astype(out_ref.dtype)


def expert_grads(near, blocks, chip, aux, gate_up, down_mat):
    rows = aux.shape[0]
    model = gate_up.shape[1]
    return pl.pallas_call(
        functools.partial(grads_kernel, near),
        out_shape=jax.ShapeDtypeStruct((rows, model + PAD), jnp.float32 if near else jnp.bfloat16),
        compiler_params=pltpu.CompilerParams(vmem_limit_bytes=16 << 20),
        cost_estimate=pl.CostEstimate(
            flops=2 * rows * model * (2 * gate_up.shape[0] + down_mat.shape[0]),
            transcendentals=rows * down_mat.shape[0],
            bytes_accessed=2 * model * (2 * rows + gate_up.shape[0] + down_mat.shape[0]),
        ),
    )(*blocks, chip, aux, gate_up, down_mat)


def body(tokens, out_grad, expert_ids, gate_weights, gate_up_rows, down_rows):
    size = lax.axis_size("expert")
    planes = size // 4
    half = planes // 2
    rows = tokens.shape[1]
    model = tokens.shape[2]
    routes = expert_ids.shape[2]
    gate_up = gate_up_rows[0, 0]
    down_mat = down_rows[0, 0]
    slots = slot_offsets(planes)

    other_in = swap(tokens[0])
    other_grad = swap(out_grad[0])
    anywhere = pl.BlockSpec(memory_space=pl.ANY)
    chip = pl.pallas_call(
        pack_kernel,
        in_specs=[anywhere] * 2 + [pl.BlockSpec(memory_space=pltpu.VMEM)] * 2,
        out_specs=anywhere,
        out_shape=jax.ShapeDtypeStruct((4,) + tokens.shape[1:], tokens.dtype),
        scratch_shapes=[pltpu.SemaphoreType.DMA((4,))],
        compiler_params=pltpu.CompilerParams(vmem_limit_bytes=1 << 20),
    )(in_hbm(tokens[0]), in_hbm(out_grad[0]), other_in, other_grad)
    held = pl.BlockSpec(memory_space=pltpu.VMEM)
    aux, gate_up, down_mat = pl.pallas_call(
        functools.partial(stage_kernel, planes, rows),
        in_specs=[held] * 2 + [anywhere] * 3,
        out_specs=[held] * 3,
        out_shape=(
            jax.ShapeDtypeStruct((size * rows, 8), jnp.float32),
            jax.ShapeDtypeStruct(gate_up.shape, gate_up.dtype),
            jax.ShapeDtypeStruct(down_mat.shape, down_mat.dtype),
        ),
        scratch_shapes=[pltpu.VMEM((size, rows, 8), jnp.float32), pltpu.SemaphoreType.DMA((2,))],
        compiler_params=pltpu.CompilerParams(vmem_limit_bytes=8 << 20),
        cost_estimate=pl.CostEstimate(
            flops=0, transcendentals=0, bytes_accessed=4 * model * (gate_up.shape[0] + down_mat.shape[0])
        ),
    )(expert_ids[0].T, gate_weights[0].T, in_hbm(gate_up), in_hbm(down_mat), chip)

    direct = [exchange(chip, *slots[k]) for k in range(half)]
    direct[0] = after(direct[0], aux)
    for k in range(half):
        direct.append(exchange(direct[k], (0, 1), (0, 1) if k < half - 1 else (0, 0)))
    gate = direct[-2]
    swapped = [swap(after(value, gate)) for value in direct[:half]] + [swap(value) for value in direct[half:]]
    near = size * rows // 2
    send = expert_grads(False, swapped, chip, aux[near:], gate_up, down_mat)
    keep = expert_grads(True, direct, chip, aux[:near], gate_up, down_mat)
    total = (keep + swap(send).astype(jnp.float32)).astype(jnp.bfloat16)
    received = [exchange(total[k * 2 * rows:(k + 1) * 2 * rows], *slots[k]) for k in range(planes)]
    total = sum(part.astype(jnp.float32) for part in received)
    final = total[:rows] + swap(total[rows:])
    grad_rows = final[:, :model].astype(jnp.bfloat16)
    lanes = final[:, model:model + 8].reshape(rows, 4, routes)
    gate_grad = jnp.sum(lanes, axis=1)
    handed = from_behind(grad_rows, "section", -1)
    return (gate_grad[None], handed[None])


def solution(mesh):
    return jax.shard_map(
        body,
        mesh=mesh,
        in_specs=(
            P("section", "expert", None),
            P("section", "expert", None),
            P("section", None, None),
            P("section", None, None),
            P("section", "expert", None, None),
            P("section", "expert", None, None),
        ),
        out_specs=(P("section", "expert", None), P("section", "expert", None)),
        check_vma=False,
    )
```

time: 227 us -> 56.6 us (0.25)
  waiting for transfers between devices: 193 us -> 22.2 us
  starting transfers between devices: 1.44 us -> 25.2 us
  between operations: 13.9 us -> 0.75 us
  matrix products: 8.71 us -> 0 us
  local copies, waits for them, and re-layouts: 7.79 us -> 2.14 us
  Pallas kernels: 0 us -> 5.37 us
    reduce_scatter x2 -> x0, waiting for transfers between devices: 116 us -> none  [the longest x1 60.5 us: body(): lax.psum_scatter(partial_value, 'expert', scatter_dimension=0, tiled=True)]
    all_gather x2 -> x0, waiting for transfers between devices: 75.3 us -> none  [the longest x1 38.2 us: body(): lax.all_gather(tokens[0], 'expert', axis=0, tiled=True)]
    ppermute x0 -> x16, starting transfers between devices: none -> 23.9 us  [the longest x8 12.4 us: exchange(): return lax.ppermute(value, 'expert', pairs)]
    ppermute x0 -> x16, waiting for transfers between devices: none -> 17.9 us  [the longest x8 13.9 us: exchange(): return lax.ppermute(value, 'expert', pairs)]
    dot_general x7 -> x0, matrix products: 8.71 us -> none  [the longest x1 3.3 us: body(): jnp.einsum('jrt,jrd->jtd', chooser, contrib.reshape(group_size, capacity,...]
    pallas_call x0 -> x4, Pallas kernels: none -> 5.37 us  [the longest x2 2.82 us: expert_grads(): pl.pallas_call(functools.partial(grads_kernel, near), out_shape=jax.Shape...]
    ppermute x1, waiting for transfers between devices: 0.01 us -> 4.29 us  [from_behind(): return lax.ppermute(shard, axis, pairs)]
    reshape x4 -> x0, local copies, waits for them, and re-layouts: 2.29 us -> none  [the longest x1 1.2 us: body(): rows_grad.reshape(-1, model_width)]
  transfers between devices with their start and end apart: 5 -> 17, of which waited for: 4 -> 13; matrix products, arithmetic and copies ran while one was open for 3% -> 1% of each run, Pallas kernels for 0% -> 5%
where the time goes in v2:
time: 56.6 us; the launch traced here: 56.4 us
  starting transfers between devices  25.2 us (45%)
  waiting for transfers between devices  22.2 us (39%)
  Pallas kernels  5.37 us (9%)
  local copies, waits for them, and re-layouts  2.14 us (4%)
  other arithmetic  0.76 us (1%)
  between operations  0.75 us (1%)
    ppermute x8, waiting for transfers between devices, exchange(): return lax.ppermute(value, 'expert', pairs)  13.9 us
    ppermute x8, starting transfers between devices, exchange(): return lax.ppermute(value, 'expert', pairs)  12.4 us
    ppermute x8, starting transfers between devices, swap(): lax.ppermute(value, 'expert', [(i, i ^ 1) for i in range(lax.axis_size('e...  11.5 us
    ppermute x1, waiting for transfers between devices, from_behind(): return lax.ppermute(shard, axis, pairs)  4.29 us
    ppermute x8, waiting for transfers between devices, swap(): lax.ppermute(value, 'expert', [(i, i ^ 1) for i in range(lax.axis_size('e...  3.94 us
    pallas_call x2, Pallas kernels, expert_grads(): pl.pallas_call(functools.partial(grads_kernel, near), out_shape=jax.Shape...  2.82 us
    unnamed x5, local copies, waits for them, and re-layouts  1.99 us
    pallas_call x1, Pallas kernels, body(): pl.pallas_call(functools.partial(stage_kernel, planes, rows), in_specs=[h...  1.64 us
  transfers between devices with their start and end apart: 17, of which 13 were waited for; matrix products, arithmetic and copies ran while one was open for 1% of the time, Pallas kernels for 5%

profile of v2, /device:TPU:0, one launch (start us, length us, event | category | flops | bytes accessed | tf_op | source)
XLA Modules:
  0.0 56.4 jit_solution(2801798327154359227)
XLA Ops:
  0.6 0.5 collective-permute-start
  1.2 1.0 %collective-permute-done.c_ref = bf16[16,2048]{1,0:T(8,128)(2,1)S(1)} collective-permute-done((bf16[16,2048]{1,0:T(8,128)(2,1)}, bf16[16,2048]{1,0:T(8,128)(2,1)S(1)}, u32[]{:S(2)}, u32[]{:S(2)}) %collective-permute-start) | collective-permute-done | bytes 65568 | tf_op jit(solution)/shard_map/ppermute | solution.py:31
  2.6 0.9 %shard_map.77._.refs_4_ = bf16[4,16,2048]{2,1,0:T(8,128)(2,1)S(1)} custom-call(bf16[16,2048]{1,0:T(8,128)(2,1)} %bitcast.19, bf16[16,2048]{1,0:T(8,128)(2,1)} %bitcast.21, bf16[16,2048]{1,0:T(8,128)(2,1)S(1)} %collective-permute-done.c_ref, bf16[16,2048]{1,0:T(8,128)(2,1)S(1)} %collective-permute-done.1.d_ref), custom_call_target="tpu_custom_call" | custom-call | tf_op jit(solution)/shard_map/pallas_call | solution.py:152
  3.5 2.8 %collective-permute-start.2 = (bf16[4,16,2048]{2,1,0:T(8,128)(2,1)S(1)}, bf16[4,16,2048]{2,1,0:T(8,128)(2,1)S(1)}, u32[]{:S(2)}, u32[]{:S(2)}) collective-permute-start(bf16[4,16,2048]{2,1,0:T(8,128)(2,1)S(1)} %shard_map.77._.refs_4_), channel_id=1, source_target_pairs={{0,4},{1,9},{2,6},{3,11},{4,0},{5,13},{6,2},{7,15},{8,12},{9,1},{1... | collective-permute-start | bytes 786440 | tf_op jit(solution)/shard_map/ppermute | solution.py:27
  6.3 1.5 %collective-permute-start.3 = (bf16[4,16,2048]{2,1,0:T(8,128)(2,1)S(1)}, bf16[4,16,2048]{2,1,0:T(8,128)(2,1)S(1)}, u32[]{:S(2)}, u32[]{:S(2)}) collective-permute-start(bf16[4,16,2048]{2,1,0:T(8,128)(2,1)S(1)} %shard_map.77._.refs_4_), channel_id=1, source_target_pairs={{0,2},{1,13},{2,0},{3,15},{4,6},{5,9},{6,4},{7,11},{8,10},{9,5},{1... | collective-permute-start | bytes 786440 | tf_op jit(solution)/shard_map/ppermute | solution.py:27
  7.8 0.7 %copy-done = s32[1,256,2]{1,2,0:T(2,128)S(1)} copy-done((s32[1,256,2]{1,2,0:T(2,128)S(1)}, s32[1,256,2]{1,2,0:T(2,128)}, u32[]{:S(2)}) %copy-start) | copy-done | bytes 2072
  8.5 0.7 %copy-done.1 = bf16[1,256,2]{1,2,0:T(2,128)(2,1)S(1)} copy-done((bf16[1,256,2]{1,2,0:T(2,128)(2,1)S(1)}, bf16[1,256,2]{1,2,0:T(2,128)(2,1)}, u32[]{:S(2)}) %copy-start.1) | copy-done | bytes 1048
  9.2 1.6 %shard_map.78 = (f32[256,8]{1,0:T(8,128)S(1)}, bf16[384,2048]{1,0:T(8,128)(2,1)S(1)}, bf16[192,2048]{1,0:T(8,128)(2,1)S(1)}) custom-call(s32[2,256]{1,0:T(2,128)S(1)} %bitcast.13, bf16[2,256]{1,0:T(2,128)(2,1)S(1)} %bitcast.14, bf16[384,2048]{1,0:T(8,128)(2,1)} %bitcast.15, bf16[192,2048]{1,0:T(8,128)(2,1)} %bitcast.16, ...), custom_call_target="tpu_custom_call" | custom-call | bytes 4718592 | tf_op jit(solution)/shard_map/pallas_call | solution.py:161
  10.9 2.2 %collective-permute-done.2.refs_0_ = bf16[4,16,2048]{2,1,0:T(8,128)(2,1)S(1)} collective-permute-done((bf16[4,16,2048]{2,1,0:T(8,128)(2,1)S(1)}, bf16[4,16,2048]{2,1,0:T(8,128)(2,1)S(1)}, u32[]{:S(2)}, u32[]{:S(2)}) %collective-permute-start.2) | collective-permute-done | bytes 262176 | tf_op jit(solution)/shard_map/ppermute | solution.py:27
  13.1 2.3 %collective-permute-start.4 = (bf16[4,16,2048]{2,1,0:T(8,128)(2,1)S(1)}, bf16[4,16,2048]{2,1,0:T(8,128)(2,1)S(1)}, u32[]{:S(2)}, u32[]{:S(2)}) collective-permute-start(bf16[4,16,2048]{2,1,0:T(8,128)(2,1)S(1)} %collective-permute-done.2.refs_0_), channel_id=1, source_target_pairs={{0,2},{1,3},{2,0},{3,1},{4,6},{5,7},{6,4},{7,5},{8,10},{9,11},{10,... | collective-permute-start | bytes 786440 | tf_op jit(solution)/shard_map/ppermute | solution.py:27
  15.4 0.7 %collective-permute-start.5 = (bf16[4,16,2048]{2,1,0:T(8,128)(2,1)S(1)}, bf16[4,16,2048]{2,1,0:T(8,128)(2,1)S(1)}, u32[]{:S(2)}, u32[]{:S(2)}) collective-permute-start(bf16[4,16,2048]{2,1,0:T(8,128)(2,1)S(1)} %collective-permute-done.3.refs_1_), channel_id=1, source_target_pairs={{0,0},{1,3},{2,2},{3,1},{4,4},{5,7},{6,6},{7,5},{8,8},{9,11},{10,1... | collective-permute-start | bytes 786440 | tf_op jit(solution)/shard_map/ppermute | solution.py:27
  16.1 5.8 %collective-permute-done.4.refs_2_ = bf16[4,16,2048]{2,1,0:T(8,128)(2,1)S(1)} collective-permute-done((bf16[4,16,2048]{2,1,0:T(8,128)(2,1)S(1)}, bf16[4,16,2048]{2,1,0:T(8,128)(2,1)S(1)}, u32[]{:S(2)}, u32[]{:S(2)}) %collective-permute-start.4) | collective-permute-done | bytes 262176 | tf_op jit(solution)/shard_map/ppermute | solution.py:27
  21.9 3.1 %collective-permute-start.9 = (bf16[4,16,2048]{2,1,0:T(8,128)(2,1)S(1)}, bf16[4,16,2048]{2,1,0:T(8,128)(2,1)S(1)}, u32[]{:S(2)}, u32[]{:S(2)}) collective-permute-start(bf16[4,16,2048]{2,1,0:T(8,128)(2,1)S(1)} %collective-permute-done.5.refs_3_), channel_id=1, source_target_pairs={{0,1},{1,0},{2,3},{3,2},{4,5},{5,4},{6,7},{7,6},{8,9},{9,8},{10,11... | collective-permute-start | bytes 786440 | tf_op jit(solution)/shard_map/ppermute | solution.py:31
  25.0 0.5 collective-permute-start.8
  25.5 0.6 %collective-permute-done.9.refs_3_ = bf16[4,16,2048]{2,1,0:T(8,128)(2,1)S(1)} collective-permute-done((bf16[4,16,2048]{2,1,0:T(8,128)(2,1)S(1)}, bf16[4,16,2048]{2,1,0:T(8,128)(2,1)S(1)}, u32[]{:S(2)}, u32[]{:S(2)}) %collective-permute-start.9) | collective-permute-done | bytes 262176 | tf_op jit(solution)/shard_map/ppermute | solution.py:31
  26.2 0.4 collective-permute-done.7.refs_1_
  26.6 0.4 collective-permute-done.8.refs_2_
  26.9 1.4 %shard_map.80 = bf16[128,2176]{1,0:T(8,128)(2,1)S(1)} custom-call(bf16[4,16,2048]{2,1,0:T(8,128)(2,1)S(1)} %collective-permute-done.6.refs_0_, bf16[4,16,2048]{2,1,0:T(8,128)(2,1)S(1)} %collective-permute-done.7.refs_1_, bf16[4,16,2048]{2,1,0:T(8,128)(2,1)S(1)} %collective-permute-done.8.refs_2_, bf16[4,16,2048]{2,1,0:T(8,128)(2,1)S(1)} %collective-permute-done.9.refs_3_, ...), custom_call_target="tpu_custom_call" | custom-call | flops 503316480 | bytes 3407872 | tf_op jit(solution)/shard_map/pallas_call | solution.py:126
  28.3 0.4 collective-permute-start.10
  28.8 1.4 %shard_map.79 = f32[128,2176]{1,0:T(8,128)S(1)} custom-call(bf16[4,16,2048]{2,1,0:T(8,128)(2,1)S(1)} %collective-permute-done.2.refs_0_, bf16[4,16,2048]{2,1,0:T(8,128)(2,1)S(1)} %collective-permute-done.3.refs_1_, bf16[4,16,2048]{2,1,0:T(8,128)(2,1)S(1)} %collective-permute-done.4.refs_2_, bf16[4,16,2048]{2,1,0:T(8,128)(2,1)S(1)} %collective-permute-done.5.refs_3_, ...), custom_call_target="tpu_custom_call" | custom-call | flops 503316480 | bytes 3407872 | tf_op jit(solution)/shard_map/pallas_call | solution.py:126
  30.5 2.8 %collective-permute-start.11 = (bf16[32,2176]{1,0:T(8,128)(2,1)S(1)}, bf16[32,2176]{1,0:T(8,128)(2,1)S(1)}, u32[]{:S(2)}, u32[]{:S(2)}) collective-permute-start(bf16[32,2176]{1,0:T(8,128)(2,1)S(1)} %get-tuple-element.14), channel_id=1, source_target_pairs={{0,4},{1,9},{2,6},{3,11},{4,0},{5,13},{6,2},{7,15},{8,12},{9,1},{1... | collective-permute-start | bytes 417800 | tf_op jit(solution)/shard_map/ppermute | solution.py:27
  33.3 0.7 %collective-permute-start.14 = (bf16[32,2176]{1,0:T(8,128)(2,1)S(1)}, bf16[32,2176]{1,0:T(8,128)(2,1)S(1)}, u32[]{:S(2)}, u32[]{:S(2)}) collective-permute-start(bf16[32,2176]{1,0:T(8,128)(2,1)S(1)} %get-tuple-element.15), channel_id=1, source_target_pairs={{0,0},{1,15},{2,2},{3,13},{4,4},{5,11},{6,6},{7,9},{8,8},{9,7},{10... | collective-permute-start | bytes 417800 | tf_op jit(solution)/shard_map/ppermute | solution.py:27
  34.0 1.0 %collective-permute-start.13 = (bf16[32,2176]{1,0:T(8,128)(2,1)S(1)}, bf16[32,2176]{1,0:T(8,128)(2,1)S(1)}, u32[]{:S(2)}, u32[]{:S(2)}) collective-permute-start(bf16[32,2176]{1,0:T(8,128)(2,1)S(1)} %get-tuple-element.16), channel_id=1, source_target_pairs={{0,6},{1,11},{2,4},{3,9},{4,2},{5,15},{6,0},{7,13},{8,14},{9,3},{1... | collective-permute-start | bytes 417800 | tf_op jit(solution)/shard_map/ppermute | solution.py:27
  35.0 0.6 %collective-permute-start.12 = (bf16[32,2176]{1,0:T(8,128)(2,1)S(1)}, bf16[32,2176]{1,0:T(8,128)(2,1)S(1)}, u32[]{:S(2)}, u32[]{:S(2)}) collective-permute-start(bf16[32,2176]{1,0:T(8,128)(2,1)S(1)} %get-tuple-element.17), channel_id=1, source_target_pairs={{0,2},{1,13},{2,0},{3,15},{4,6},{5,9},{6,4},{7,11},{8,10},{9,5},{1... | collective-permute-start | bytes 417800 | tf_op jit(solution)/shard_map/ppermute | solution.py:27
  35.6 0.7 %collective-permute-done.11 = bf16[32,2176]{1,0:T(8,128)(2,1)S(1)} collective-permute-done((bf16[32,2176]{1,0:T(8,128)(2,1)S(1)}, bf16[32,2176]{1,0:T(8,128)(2,1)S(1)}, u32[]{:S(2)}, u32[]{:S(2)}) %collective-permute-start.11) | collective-permute-done | bytes 139296 | tf_op jit(solution)/shard_map/ppermute | solution.py:27
  36.4 5.0 %collective-permute-done.13 = bf16[32,2176]{1,0:T(8,128)(2,1)S(1)} collective-permute-done((bf16[32,2176]{1,0:T(8,128)(2,1)S(1)}, bf16[32,2176]{1,0:T(8,128)(2,1)S(1)}, u32[]{:S(2)}, u32[]{:S(2)}) %collective-permute-start.13) | collective-permute-done | bytes 139296 | tf_op jit(solution)/shard_map/ppermute | solution.py:27
  41.6 6.9 %collective-permute-start.15 = (f32[16,2176]{1,0:T(8,128)S(1)}, f32[16,2176]{1,0:T(8,128)S(1)}, u32[]{:S(2)}, u32[]{:S(2)}) collective-permute-start(f32[16,2176]{1,0:T(8,128)S(1)} %slice.46), channel_id=1, source_target_pairs={{0,1},{1,0},{2,3},{3,2},{4,5},{5,4},{6,7},{7,6},{8,9},{9,8},{10,11... | collective-permute-start | bytes 417800 | tf_op jit(solution)/shard_map/ppermute | solution.py:31
  48.4 1.0 %collective-permute-done.15 = f32[16,2176]{1,0:T(8,128)S(1)} collective-permute-done((f32[16,2176]{1,0:T(8,128)S(1)}, f32[16,2176]{1,0:T(8,128)S(1)}, u32[]{:S(2)}, u32[]{:S(2)}) %collective-permute-start.15) | collective-permute-done | bytes 139296 | tf_op jit(solution)/shard_map/ppermute | solution.py:31
  49.5 1.3 %collective-permute-start.16 = (bf16[16,2048]{1,0:T(8,128)(2,1)S(1)}, bf16[16,2048]{1,0:T(8,128)(2,1)S(1)}, u32[]{:S(2)}, u32[]{:S(2)}) collective-permute-start(bf16[16,2048]{1,0:T(8,128)(2,1)S(1)} %slice.51), channel_id=1, source_target_pairs={{16,0},{17,1},{18,2},{19,3},{20,4},{21,5},{22,6},{23,7},{24,8},{25... | collective-permute-start | bytes 196616 | tf_op jit(solution)/shard_map/ppermute | solution.py:37
  50.9 0.6 %reduce_sum.9 = f32[16,2]{0,1:T(2,128)} reduce(f32[16,4,2]{0,2,1:T(2,128)S(1)} %bitcast.22, f32[]{:T(128)} %constant.0.clone.1), dimensions={1}, to_apply=%region_0.0 | reduce | flops 96 | bytes 644 | tf_op jit(solution)/shard_map/reduce_sum | solution.py:192
  51.4 4.3 %collective-permute-done.16 = bf16[16,2048]{1,0:T(8,128)(2,1)S(1)} collective-permute-done((bf16[16,2048]{1,0:T(8,128)(2,1)S(1)}, bf16[16,2048]{1,0:T(8,128)(2,1)S(1)}, u32[]{:S(2)}, u32[]{:S(2)}) %collective-permute-start.16) | collective-permute-done | bytes 65568 | tf_op jit(solution)/shard_map/ppermute | solution.py:37
  55.7 0.6 %copy.10 = bf16[1,16,2048]{2,1,0:T(8,128)(2,1)} copy(bf16[1,16,2048]{2,1,0:T(8,128)(2,1)S(1)} %bitcast.17) | data formatting | bytes 131072
  (21 shorter events, 1.1 us)
Async XLA Ops:
  0.6 1.6 %collective-permute-start = (bf16[16,2048]{1,0:T(8,128)(2,1)}, bf16[16,2048]{1,0:T(8,128)(2,1)S(1)}, u32[]{:S(2)}, u32[]{:S(2)}) collective-permute-start(bf16[16,2048]{1,0:T(8,128)(2,1)} %bitcast.18), channel_id=1, source_target_pairs={{0,1},{1,0},{2,3},{3,2},{4,5},{5,4},{6,7},{7,6},{8,9},{9,8},{10,11... | collective-permute-start | bytes 196616 | tf_op jit(solution)/shard_map/ppermute | solution.py:31
  1.1 1.5 %collective-permute-start.1 = (bf16[16,2048]{1,0:T(8,128)(2,1)}, bf16[16,2048]{1,0:T(8,128)(2,1)S(1)}, u32[]{:S(2)}, u32[]{:S(2)}) collective-permute-start(bf16[16,2048]{1,0:T(8,128)(2,1)} %bitcast.20), channel_id=1, source_target_pairs={{0,1},{1,0},{2,3},{3,2},{4,5},{5,4},{6,7},{7,6},{8,9},{9,8},{10,11... | collective-permute-start | bytes 196616 | tf_op jit(solution)/shard_map/ppermute | solution.py:31
  3.5 9.5 %collective-permute-start.2 = (bf16[4,16,2048]{2,1,0:T(8,128)(2,1)S(1)}, bf16[4,16,2048]{2,1,0:T(8,128)(2,1)S(1)}, u32[]{:S(2)}, u32[]{:S(2)}) collective-permute-start(bf16[4,16,2048]{2,1,0:T(8,128)(2,1)S(1)} %shard_map.77._.refs_4_), channel_id=1, source_target_pairs={{0,4},{1,9},{2,6},{3,11},{4,0},{5,13},{6,2},{7,15},{8,12},{9,1},{1... | collective-permute-start | bytes 786440 | tf_op jit(solution)/shard_map/ppermute | solution.py:27
  6.3 9.1 %collective-permute-start.3 = (bf16[4,16,2048]{2,1,0:T(8,128)(2,1)S(1)}, bf16[4,16,2048]{2,1,0:T(8,128)(2,1)S(1)}, u32[]{:S(2)}, u32[]{:S(2)}) collective-permute-start(bf16[4,16,2048]{2,1,0:T(8,128)(2,1)S(1)} %shard_map.77._.refs_4_), channel_id=1, source_target_pairs={{0,2},{1,13},{2,0},{3,15},{4,6},{5,9},{6,4},{7,11},{8,10},{9,5},{1... | collective-permute-start | bytes 786440 | tf_op jit(solution)/shard_map/ppermute | solution.py:27
  7.8 0.7 %copy-start = (s32[1,256,2]{1,2,0:T(2,128)S(1)}, s32[1,256,2]{1,2,0:T(2,128)}, u32[]{:S(2)}) copy-start(s32[1,256,2]{1,2,0:T(2,128)} %param.8) | copy-start | bytes 6148
  8.5 0.7 %copy-start.1 = (bf16[1,256,2]{1,2,0:T(2,128)(2,1)S(1)}, bf16[1,256,2]{1,2,0:T(2,128)(2,1)}, u32[]{:S(2)}) copy-start(bf16[1,256,2]{1,2,0:T(2,128)(2,1)} %param.9) | copy-start | bytes 3076
  13.1 8.8 %collective-permute-start.4 = (bf16[4,16,2048]{2,1,0:T(8,128)(2,1)S(1)}, bf16[4,16,2048]{2,1,0:T(8,128)(2,1)S(1)}, u32[]{:S(2)}, u32[]{:S(2)}) collective-permute-start(bf16[4,16,2048]{2,1,0:T(8,128)(2,1)S(1)} %collective-permute-done.2.refs_0_), channel_id=1, source_target_pairs={{0,2},{1,3},{2,0},{3,1},{4,6},{5,7},{6,4},{7,5},{8,10},{9,11},{10,... | collective-permute-start | bytes 786440 | tf_op jit(solution)/shard_map/ppermute | solution.py:27
  15.4 6.5 %collective-permute-start.5 = (bf16[4,16,2048]{2,1,0:T(8,128)(2,1)S(1)}, bf16[4,16,2048]{2,1,0:T(8,128)(2,1)S(1)}, u32[]{:S(2)}, u32[]{:S(2)}) collective-permute-start(bf16[4,16,2048]{2,1,0:T(8,128)(2,1)S(1)} %collective-permute-done.3.refs_1_), channel_id=1, source_target_pairs={{0,0},{1,3},{2,2},{3,1},{4,4},{5,7},{6,6},{7,5},{8,8},{9,11},{10,1... | collective-permute-start | bytes 786440 | tf_op jit(solution)/shard_map/ppermute | solution.py:27
  21.9 4.3 %collective-permute-start.6 = (bf16[4,16,2048]{2,1,0:T(8,128)(2,1)S(1)}, bf16[4,16,2048]{2,1,0:T(8,128)(2,1)S(1)}, u32[]{:S(2)}, u32[]{:S(2)}) collective-permute-start(bf16[4,16,2048]{2,1,0:T(8,128)(2,1)S(1)} %collective-permute-done.2.refs_0_), channel_id=1, source_target_pairs={{0,1},{1,0},{2,3},{3,2},{4,5},{5,4},{6,7},{7,6},{8,9},{9,8},{10,11... | collective-permute-start | bytes 786440 | tf_op jit(solution)/shard_map/ppermute | solution.py:31
  21.9 4.3 %collective-permute-start.9 = (bf16[4,16,2048]{2,1,0:T(8,128)(2,1)S(1)}, bf16[4,16,2048]{2,1,0:T(8,128)(2,1)S(1)}, u32[]{:S(2)}, u32[]{:S(2)}) collective-permute-start(bf16[4,16,2048]{2,1,0:T(8,128)(2,1)S(1)} %collective-permute-done.5.refs_3_), channel_id=1, source_target_pairs={{0,1},{1,0},{2,3},{3,2},{4,5},{5,4},{6,7},{7,6},{8,9},{9,8},{10,11... | collective-permute-start | bytes 786440 | tf_op jit(solution)/shard_map/ppermute | solution.py:31
  25.0 1.5 %collective-permute-start.7 = (bf16[4,16,2048]{2,1,0:T(8,128)(2,1)S(1)}, bf16[4,16,2048]{2,1,0:T(8,128)(2,1)S(1)}, u32[]{:S(2)}, u32[]{:S(2)}) collective-permute-start(bf16[4,16,2048]{2,1,0:T(8,128)(2,1)S(1)} %collective-permute-done.3.refs_1_), channel_id=1, source_target_pairs={{0,1},{1,0},{2,3},{3,2},{4,5},{5,4},{6,7},{7,6},{8,9},{9,8},{10,11... | collective-permute-start | bytes 786440 | tf_op jit(solution)/shard_map/ppermute | solution.py:31
  25.0 1.9 %collective-permute-start.8 = (bf16[4,16,2048]{2,1,0:T(8,128)(2,1)S(1)}, bf16[4,16,2048]{2,1,0:T(8,128)(2,1)S(1)}, u32[]{:S(2)}, u32[]{:S(2)}) collective-permute-start(bf16[4,16,2048]{2,1,0:T(8,128)(2,1)S(1)} %collective-permute-done.4.refs_2_), channel_id=1, source_target_pairs={{0,1},{1,0},{2,3},{3,2},{4,5},{5,4},{6,7},{7,6},{8,9},{9,8},{10,11... | collective-permute-start | bytes 786440 | tf_op jit(solution)/shard_map/ppermute | solution.py:31
  28.3 2.0 %collective-permute-start.10 = (bf16[128,2176]{1,0:T(8,128)(2,1)S(1)}, bf16[128,2176]{1,0:T(8,128)(2,1)S(1)}, u32[]{:S(2)}, u32[]{:S(2)}) collective-permute-start(bf16[128,2176]{1,0:T(8,128)(2,1)S(1)} %shard_map.80), channel_id=1, source_target_pairs={{0,1},{1,0},{2,3},{3,2},{4,5},{5,4},{6,7},{7,6},{8,9},{9,8},{10,11... | collective-permute-start | bytes 1671176 | tf_op jit(solution)/shard_map/ppermute | solution.py:31
  30.5 5.8 %collective-permute-start.11 = (bf16[32,2176]{1,0:T(8,128)(2,1)S(1)}, bf16[32,2176]{1,0:T(8,128)(2,1)S(1)}, u32[]{:S(2)}, u32[]{:S(2)}) collective-permute-start(bf16[32,2176]{1,0:T(8,128)(2,1)S(1)} %get-tuple-element.14), channel_id=1, source_target_pairs={{0,4},{1,9},{2,6},{3,11},{4,0},{5,13},{6,2},{7,15},{8,12},{9,1},{1... | collective-permute-start | bytes 417800 | tf_op jit(solution)/shard_map/ppermute | solution.py:27
  33.3 3.0 %collective-permute-start.14 = (bf16[32,2176]{1,0:T(8,128)(2,1)S(1)}, bf16[32,2176]{1,0:T(8,128)(2,1)S(1)}, u32[]{:S(2)}, u32[]{:S(2)}) collective-permute-start(bf16[32,2176]{1,0:T(8,128)(2,1)S(1)} %get-tuple-element.15), channel_id=1, source_target_pairs={{0,0},{1,15},{2,2},{3,13},{4,4},{5,11},{6,6},{7,9},{8,8},{9,7},{10... | collective-permute-start | bytes 417800 | tf_op jit(solution)/shard_map/ppermute | solution.py:27
  34.0 7.4 %collective-permute-start.13 = (bf16[32,2176]{1,0:T(8,128)(2,1)S(1)}, bf16[32,2176]{1,0:T(8,128)(2,1)S(1)}, u32[]{:S(2)}, u32[]{:S(2)}) collective-permute-start(bf16[32,2176]{1,0:T(8,128)(2,1)S(1)} %get-tuple-element.16), channel_id=1, source_target_pairs={{0,6},{1,11},{2,4},{3,9},{4,2},{5,15},{6,0},{7,13},{8,14},{9,3},{1... | collective-permute-start | bytes 417800 | tf_op jit(solution)/shard_map/ppermute | solution.py:27
  35.0 6.5 %collective-permute-start.12 = (bf16[32,2176]{1,0:T(8,128)(2,1)S(1)}, bf16[32,2176]{1,0:T(8,128)(2,1)S(1)}, u32[]{:S(2)}, u32[]{:S(2)}) collective-permute-start(bf16[32,2176]{1,0:T(8,128)(2,1)S(1)} %get-tuple-element.17), channel_id=1, source_target_pairs={{0,2},{1,13},{2,0},{3,15},{4,6},{5,9},{6,4},{7,11},{8,10},{9,5},{1... | collective-permute-start | bytes 417800 | tf_op jit(solution)/shard_map/ppermute | solution.py:27
  41.6 7.9 %collective-permute-start.15 = (f32[16,2176]{1,0:T(8,128)S(1)}, f32[16,2176]{1,0:T(8,128)S(1)}, u32[]{:S(2)}, u32[]{:S(2)}) collective-permute-start(f32[16,2176]{1,0:T(8,128)S(1)} %slice.46), channel_id=1, source_target_pairs={{0,1},{1,0},{2,3},{3,2},{4,5},{5,4},{6,7},{7,6},{8,9},{9,8},{10,11... | collective-permute-start | bytes 417800 | tf_op jit(solution)/shard_map/ppermute | solution.py:31
  49.5 6.3 %collective-permute-start.16 = (bf16[16,2048]{1,0:T(8,128)(2,1)S(1)}, bf16[16,2048]{1,0:T(8,128)(2,1)S(1)}, u32[]{:S(2)}, u32[]{:S(2)}) collective-permute-start(bf16[16,2048]{1,0:T(8,128)(2,1)S(1)} %slice.51), channel_id=1, source_target_pairs={{16,0},{17,1},{18,2},{19,3},{20,4},{21,5},{22,6},{23,7},{24,8},{25... | collective-permute-start | bytes 196616 | tf_op jit(solution)/shard_map/ppermute | solution.py:37

commit v3 on v2

v3 whole, which is shorter than its diff:
```python
import functools

import jax
import jax.numpy as jnp
from jax import lax
from jax.experimental import pallas as pl
from jax.experimental.pallas import tpu as pltpu
from jax.sharding import PartitionSpec as P

PAD = 128


def slot_offsets(planes):
    half = planes // 2
    far = [(half + k, 0) for k in range(half)]
    near = [(k + 1, 0) for k in range(half - 1)] + [(0, 1)]
    slots = list(zip(far, near))
    return slots + [((a[0], 1), (b[0], 1 - b[1])) for a, b in slots]


def exchange(value, ahead, behind):
    pairs = []
    for here in range(lax.axis_size("expert")):
        z, y, c = here // 4, here // 2 % 2, here % 2
        dz, dy = ahead if c else behind
        pairs.append((here, (z ^ dz) * 4 + (y ^ dy) * 2 + c))
    return lax.ppermute(value, "expert", pairs)


def swap(value):
    return lax.ppermute(value, "expert", [(i, i ^ 1) for i in range(lax.axis_size("expert"))])


def from_behind(shard, axis, by):
    length = lax.axis_size(axis)
    pairs = [(i, i + by) for i in range(length) if 0 <= i + by < length]
    return lax.ppermute(shard, axis, pairs)


def after(value, *others):
    return lax.optimization_barrier((value,) + others)[0]


def in_hbm(value):
    return pltpu.with_memory_space_constraint(value, pltpu.HBM)


def load_kernel(a_ref, b_ref, out_ref, sems):
    copies = [pltpu.make_async_copy(ref, out_ref.at[i], sems.at[i]) for i, ref in enumerate((a_ref, b_ref))]
    for copy in copies:
        copy.start()
    for copy in copies:
        copy.wait()


def pack_kernel(own_ref, a_ref, b_ref, out_ref):
    out_ref[0:2] = own_ref[...]
    out_ref[2] = a_ref[...]
    out_ref[3] = b_ref[...]


def stage_kernel(planes, rows, ids_ref, gates_ref, up_ref, down_ref, _, out_ref, up_out, up_flip, down_flip, gate_ref, down_out, sems):
    copies = [
        pltpu.make_async_copy(up_ref, up_out, sems.at[0]),
        pltpu.make_async_copy(down_ref, down_out, sems.at[1]),
    ]
    for copy in copies:
        copy.start()
    position = lax.axis_index("expert")
    z, y, c = position // 4, position // 2 % 2, position % 2
    expert = position // (4 * planes // max(2, planes))
    match = (ids_ref[...] == expert).astype(jnp.float32)
    gate = jnp.sum(match * gates_ref[...].astype(jnp.float32), axis=0, keepdims=True)
    table = jnp.concatenate([gate, match, jnp.zeros((8 - 1 - match.shape[0], gate.shape[1]), jnp.float32)], axis=0)
    columns = jnp.transpose(table)
    gate_ref[...] = columns.reshape(gate_ref.shape)
    at = 0
    half = planes // 2
    slots = slot_offsets(planes)
    for core, group in ((c, slots[:half]), (c ^ 1, slots[:half]), (c, slots[half:]), (c ^ 1, slots[half:])):
        for ahead, behind in group:
            dz = jnp.where(core == 1, ahead[0], behind[0])
            dy = jnp.where(core == 1, ahead[1], behind[1])
            chip = (z ^ dz) * 2 + (y ^ dy)
            for unit in (0, 1):
                out_ref[at:at + rows] = gate_ref[chip * 2 + (core ^ unit)]
                at += rows
    for copy in copies:
        copy.wait()
    up_flip[...] = jnp.transpose(up_out[...])
    down_flip[...] = jnp.transpose(down_out[...])


def grads_kernel(count, own, *refs):
    blocks, (aux_ref, gate_up_ref, up_flip_ref, down_flip_ref, keep_ref, send_ref) = refs[:count], refs[-6:]
    width = down_flip_ref.shape[1]
    model = gate_up_ref.shape[1]
    near = keep_ref.shape[0]
    units = [[ref[i] for i in range(4)] for ref in blocks]
    if own:
        odd_core = lax.axis_index("expert") % 2 == 1
        chip = [refs[count][i] for i in range(4)]
        units[count // 2 - 1] = [jnp.where(odd_core, a, b) for a, b in zip(units[count // 2 - 1], chip)]
        units[-1] = [jnp.where(odd_core, b, a) for a, b in zip(units[-1], chip[2:] + chip[:2])]
    rows_in = jnp.concatenate([unit[i] for unit in units for i in (0, 2)], axis=0)
    rows_grad = jnp.concatenate([unit[i] for unit in units for i in (1, 3)], axis=0)
    both = jnp.dot(rows_in, up_flip_ref[...], preferred_element_type=jnp.float32)
    back = jnp.dot(rows_grad, down_flip_ref[...], preferred_element_type=jnp.float32)
    first = both[:, :width]
    second = both[:, width:]
    sigma = jax.nn.sigmoid(first)
    active = first * sigma
    gate = aux_ref[:, 0:1]
    slot_grad = jnp.sum(back * active * second, axis=1, keepdims=True)
    scaled = gate * back
    d_first = scaled * second * sigma * (1.0 + first * (1.0 - sigma))
    d_second = scaled * active
    d_both = jnp.concatenate([d_first, d_second], axis=1).astype(jnp.bfloat16)
    contrib = jnp.dot(d_both, gate_up_ref[...], preferred_element_type=jnp.float32)
    keep_ref[:, :model] = contrib[:near]
    send_ref[:, :model] = contrib[near:].astype(jnp.bfloat16)
    rows = slot_grad.shape[0]
    lane = lax.broadcasted_iota(jnp.int32, (rows, PAD), 1)
    row = lax.broadcasted_iota(jnp.int32, (rows, PAD), 0)
    picked = jnp.where(lane % 2 == 0, aux_ref[:, 1:2], aux_ref[:, 2:3]) * slot_grad
    high = picked.astype(jnp.bfloat16).astype(jnp.float32)
    place = lane - jnp.where(row < near, 0, 4)
    packed = jnp.where(place // 2 == 0, high, jnp.where(place // 2 == 1, picked - high, 0.0))
    keep_ref[:, model:] = packed[:near]
    send_ref[:, model:] = packed[near:].astype(jnp.bfloat16)


def expert_grads(blocks, own, aux, weights):
    rows = aux.shape[0]
    width, model = weights[0].shape
    return pl.pallas_call(
        functools.partial(grads_kernel, len(blocks), bool(own)),
        out_shape=(
            jax.ShapeDtypeStruct((rows // 2, model + PAD), jnp.float32),
            jax.ShapeDtypeStruct((rows // 2, model + PAD), jnp.bfloat16),
        ),
        compiler_params=pltpu.CompilerParams(vmem_limit_bytes=16 << 20),
        cost_estimate=pl.CostEstimate(
            flops=5 * rows * model * width,
            transcendentals=rows * width // 2,
            bytes_accessed=2 * model * (2 * rows) + 3 * model * width,
        ),
    )(*blocks, *own, aux, *weights)


def body(tokens, out_grad, expert_ids, gate_weights, gate_up_rows, down_rows):
    size = lax.axis_size("expert")
    planes = size // 4
    half = planes // 2
    rows = tokens.shape[1]
    model = tokens.shape[2]
    routes = expert_ids.shape[2]
    gate_up = gate_up_rows[0, 0]
    down_mat = down_rows[0, 0]
    slots = slot_offsets(planes)

    other_in = swap(tokens[0])
    other_grad = swap(out_grad[0])
    anywhere = pl.BlockSpec(memory_space=pl.ANY)
    held = pl.BlockSpec(memory_space=pltpu.VMEM)
    own = pl.pallas_call(
        load_kernel,
        in_specs=[anywhere] * 2,
        out_specs=held,
        out_shape=jax.ShapeDtypeStruct((2,) + tokens.shape[1:], tokens.dtype),
        scratch_shapes=[pltpu.SemaphoreType.DMA((2,))],
        compiler_params=pltpu.CompilerParams(vmem_limit_bytes=1 << 20),
    )(in_hbm(tokens[0]), in_hbm(out_grad[0]))
    chip = pl.pallas_call(
        pack_kernel,
        in_specs=[held] * 3,
        out_specs=held,
        out_shape=jax.ShapeDtypeStruct((4,) + tokens.shape[1:], tokens.dtype),
        compiler_params=pltpu.CompilerParams(vmem_limit_bytes=1 << 20),
    )(own, other_in, other_grad)
    aux, *weights = pl.pallas_call(
        functools.partial(stage_kernel, planes, rows),
        in_specs=[held] * 2 + [anywhere] * 3,
        out_specs=[held] * 4,
        out_shape=(
            jax.ShapeDtypeStruct((size * rows, 8), jnp.float32),
            jax.ShapeDtypeStruct(gate_up.shape, gate_up.dtype),
            jax.ShapeDtypeStruct(gate_up.shape[::-1], gate_up.dtype),
            jax.ShapeDtypeStruct(down_mat.shape[::-1], down_mat.dtype),
        ),
        scratch_shapes=[
            pltpu.VMEM((size, rows, 8), jnp.float32),
            pltpu.VMEM(down_mat.shape, down_mat.dtype),
            pltpu.SemaphoreType.DMA((2,)),
        ],
        compiler_params=pltpu.CompilerParams(vmem_limit_bytes=16 << 20),
        cost_estimate=pl.CostEstimate(
            flops=0, transcendentals=0, bytes_accessed=4 * model * (gate_up.shape[0] + down_mat.shape[0])
        ),
    )(expert_ids[0].T, gate_weights[0].T, in_hbm(gate_up), in_hbm(down_mat), chip)

    first = [exchange(chip, *slots[k]) for k in range(half)]
    first[0] = after(first[0], aux)
    then = [exchange(first[k], (0, 1), (0, 1) if k < half - 1 else (0, 0)) for k in range(half)]
    swapped = [swap(after(value, first[-1])) for value in first[:-1]] + [swap(after(first[-1], then[0]))]
    near = size * rows // 2
    keep, send1 = expert_grads(first + swapped, [], aux[:near], weights)
    came = after(swap(send1), then[-1])
    total1 = (keep + came.astype(jnp.float32)).astype(jnp.bfloat16)
    late = [value for value in then[:-1]]
    late.append(then[-1])
    swapped = [swap(value) for value in late]
    keep, send = expert_grads(late + swapped, [chip], aux[near:], weights)
    total = (keep + swap(send).astype(jnp.float32)).astype(jnp.bfloat16)
    received = [exchange(total1[k * 2 * rows:(k + 1) * 2 * rows], *slots[k]) for k in range(half)]
    received += [exchange(total[k * 2 * rows:(k + 1) * 2 * rows], *slots[half + k]) for k in range(half)]
    total = sum(part.astype(jnp.float32) for part in received)
    final = total[:rows] + swap(total[rows:])
    grad_rows = final[:, :model].astype(jnp.bfloat16)
    lanes = final[:, model:model + 8].reshape(rows, 4, routes)
    gate_grad = jnp.sum(lanes, axis=1)
    handed = from_behind(grad_rows, "section", -1)
    return (gate_grad[None], handed[None])


def solution(mesh):
    return jax.shard_map(
        body,
        mesh=mesh,
        in_specs=(
            P("section", "expert", None),
            P("section", "expert", None),
            P("section", None, None),
            P("section", None, None),
            P("section", "expert", None, None),
            P("section", "expert", None, None),
        ),
        out_specs=(P("section", "expert", None), P("section", "expert", None)),
        check_vma=False,
    )
```

time: 56.6 us -> 52 us (0.919)
  waiting for transfers between devices: 22.2 us -> 16.7 us
    ppermute x8, waiting for transfers between devices: 13.9 us -> 10.9 us  [exchange(): return lax.ppermute(value, 'expert', pairs)]
    ppermute x8 -> x9, waiting for transfers between devices: 3.94 us -> 1.5 us  [swap(): lax.ppermute(value, 'expert', [(i, i ^ 1) for i in range(lax.axis_size('e...]
    pallas_call x1, Pallas kernels: 1.64 us -> 2.38 us  [body(): pl.pallas_call(functools.partial(stage_kernel, planes, rows), in_specs=[h...]
    pallas_call x3 -> x4, Pallas kernels: 3.73 us -> 3.47 us  [the longest x2 2.57 us: expert_grads(): pl.pallas_call(functools.partial(grads_kernel, len(blocks), bool(own)), o...]
    ppermute x8 -> x9, starting transfers between devices: 11.5 us -> 11.4 us  [swap(): lax.ppermute(value, 'expert', [(i, i ^ 1) for i in range(lax.axis_size('e...]
  transfers between devices with their start and end apart: 17 -> 18, of which waited for: 13 -> 8; matrix products, arithmetic and copies ran while one was open for 1% -> 2% of each run, Pallas kernels for 5% -> 11%
where the time goes in v3:
time: 52 us; the launch traced here: 51.7 us
  starting transfers between devices  25.5 us (49%)
  waiting for transfers between devices  16.7 us (32%)
  Pallas kernels  5.86 us (11%)
  local copies, waits for them, and re-layouts  2.13 us (4%)
  between operations  0.79 us (2%)
  other arithmetic  0.78 us (2%)
    ppermute x8, starting transfers between devices, exchange(): return lax.ppermute(value, 'expert', pairs)  12.8 us
    ppermute x9, starting transfers between devices, swap(): lax.ppermute(value, 'expert', [(i, i ^ 1) for i in range(lax.axis_size('e...  11.4 us
    ppermute x8, waiting for transfers between devices, exchange(): return lax.ppermute(value, 'expert', pairs)  10.9 us
    ppermute x1, waiting for transfers between devices, from_behind(): return lax.ppermute(shard, axis, pairs)  4.29 us
    pallas_call x2, Pallas kernels, expert_grads(): pl.pallas_call(functools.partial(grads_kernel, len(blocks), bool(own)), o...  2.57 us
    pallas_call x1, Pallas kernels, body(): pl.pallas_call(functools.partial(stage_kernel, planes, rows), in_specs=[h...  2.38 us
    unnamed x5, local copies, waits for them, and re-layouts  1.99 us
    ppermute x9, waiting for transfers between devices, swap(): lax.ppermute(value, 'expert', [(i, i ^ 1) for i in range(lax.axis_size('e...  1.5 us
  transfers between devices with their start and end apart: 18, of which 8 were waited for; matrix products, arithmetic and copies ran while one was open for 2% of the time, Pallas kernels for 11%

profile of v3, /device:TPU:0, one launch (start us, length us, event | category | flops | bytes accessed | tf_op | source)
XLA Modules:
  0.0 51.7 jit_solution(14699691173567288460)
XLA Ops:
  0.6 0.5 %collective-permute-start = (bf16[16,2048]{1,0:T(8,128)(2,1)}, bf16[16,2048]{1,0:T(8,128)(2,1)S(1)}, u32[]{:S(2)}, u32[]{:S(2)}) collective-permute-start(bf16[16,2048]{1,0:T(8,128)(2,1)} %bitcast.18), channel_id=1, source_target_pairs={{0,1},{1,0},{2,3},{3,2},{4,5},{5,4},{6,7},{7,6},{8,9},{9,8},{10,11... | collective-permute-start | bytes 196616 | tf_op jit(solution)/shard_map/ppermute | solution.py:31
  1.1 0.1 collective-permute-start.1
  1.2 0.9 %shard_map.77.own_ref = bf16[2,16,2048]{2,1,0:T(8,128)(2,1)S(1)} custom-call(bf16[16,2048]{1,0:T(8,128)(2,1)} %bitcast.19, bf16[16,2048]{1,0:T(8,128)(2,1)} %bitcast.21), custom_call_target="tpu_custom_call" | custom-call | tf_op jit(solution)/shard_map/pallas_call | solution.py:166
  2.1 0.1 collective-permute-done.a_ref
  2.3 0.4 collective-permute-done.1.b_ref
  2.6 2.8 %collective-permute-start.2 = (bf16[4,16,2048]{2,1,0:T(8,128)(2,1)S(1)}, bf16[4,16,2048]{2,1,0:T(8,128)(2,1)S(1)}, u32[]{:S(2)}, u32[]{:S(2)}) collective-permute-start(bf16[4,16,2048]{2,1,0:T(8,128)(2,1)S(1)} %shard_map.78._.refs_4_), channel_id=1, source_target_pairs={{0,4},{1,9},{2,6},{3,11},{4,0},{5,13},{6,2},{7,15},{8,12},{9,1},{1... | collective-permute-start | bytes 786440 | tf_op jit(solution)/shard_map/ppermute | solution.py:27
  5.4 1.5 %collective-permute-start.3 = (bf16[4,16,2048]{2,1,0:T(8,128)(2,1)S(1)}, bf16[4,16,2048]{2,1,0:T(8,128)(2,1)S(1)}, u32[]{:S(2)}, u32[]{:S(2)}) collective-permute-start(bf16[4,16,2048]{2,1,0:T(8,128)(2,1)S(1)} %shard_map.78._.refs_4_), channel_id=1, source_target_pairs={{0,2},{1,13},{2,0},{3,15},{4,6},{5,9},{6,4},{7,11},{8,10},{9,5},{1... | collective-permute-start | bytes 786440 | tf_op jit(solution)/shard_map/ppermute | solution.py:27
  7.0 0.7 %copy-done = s32[1,256,2]{1,2,0:T(2,128)S(1)} copy-done((s32[1,256,2]{1,2,0:T(2,128)S(1)}, s32[1,256,2]{1,2,0:T(2,128)}, u32[]{:S(2)}) %copy-start) | copy-done | bytes 2072
  7.6 0.7 %copy-done.1 = bf16[1,256,2]{1,2,0:T(2,128)(2,1)S(1)} copy-done((bf16[1,256,2]{1,2,0:T(2,128)(2,1)S(1)}, bf16[1,256,2]{1,2,0:T(2,128)(2,1)}, u32[]{:S(2)}) %copy-start.1) | copy-done | bytes 1048
  8.3 2.4 %shard_map.79 = (f32[256,8]{1,0:T(8,128)S(1)}, bf16[384,2048]{1,0:T(8,128)(2,1)S(1)}, bf16[2048,384]{1,0:T(8,128)(2,1)S(1)}, bf16[2048,192]{1,0:T(8,128)(2,1)S(1)}) custom-call(s32[2,256]{1,0:T(2,128)S(1)} %bitcast.13, bf16[2,256]{1,0:T(2,128)(2,1)S(1)} %bitcast.14, bf16[384,2048]{1,0:T(8,128)(2,1)} %bitcast.15, bf16[192,2048]{1,0:T(8,128)(2,1)} %bitcast.16, ...), custom_call_target="tpu_custom_call" | custom-call | bytes 4718592 | tf_op jit(solution)/shard_map/pallas_call | solution.py:181
  10.7 1.5 %collective-permute-done.2.refs_0_ = bf16[4,16,2048]{2,1,0:T(8,128)(2,1)S(1)} collective-permute-done((bf16[4,16,2048]{2,1,0:T(8,128)(2,1)S(1)}, bf16[4,16,2048]{2,1,0:T(8,128)(2,1)S(1)}, u32[]{:S(2)}, u32[]{:S(2)}) %collective-permute-start.2) | collective-permute-done | bytes 262176 | tf_op jit(solution)/shard_map/ppermute | solution.py:27
  12.2 2.3 %collective-permute-start.5 = (bf16[4,16,2048]{2,1,0:T(8,128)(2,1)S(1)}, bf16[4,16,2048]{2,1,0:T(8,128)(2,1)S(1)}, u32[]{:S(2)}, u32[]{:S(2)}) collective-permute-start(bf16[4,16,2048]{2,1,0:T(8,128)(2,1)S(1)} %collective-permute-done.2.refs_0_), channel_id=1, source_target_pairs={{0,2},{1,3},{2,0},{3,1},{4,6},{5,7},{6,4},{7,5},{8,10},{9,11},{10,... | collective-permute-start | bytes 786440 | tf_op jit(solution)/shard_map/ppermute | solution.py:27
  14.5 2.5 %collective-permute-start.4 = (bf16[4,16,2048]{2,1,0:T(8,128)(2,1)S(1)}, bf16[4,16,2048]{2,1,0:T(8,128)(2,1)S(1)}, u32[]{:S(2)}, u32[]{:S(2)}) collective-permute-start(bf16[4,16,2048]{2,1,0:T(8,128)(2,1)S(1)} %collective-permute-done.2.refs_0_), channel_id=1, source_target_pairs={{0,1},{1,0},{2,3},{3,2},{4,5},{5,4},{6,7},{7,6},{8,9},{9,8},{10,11... | collective-permute-start | bytes 786440 | tf_op jit(solution)/shard_map/ppermute | solution.py:31
  17.0 0.7 %collective-permute-start.8 = (bf16[4,16,2048]{2,1,0:T(8,128)(2,1)S(1)}, bf16[4,16,2048]{2,1,0:T(8,128)(2,1)S(1)}, u32[]{:S(2)}, u32[]{:S(2)}) collective-permute-start(bf16[4,16,2048]{2,1,0:T(8,128)(2,1)S(1)} %collective-permute-done.3.refs_1_), channel_id=1, source_target_pairs={{0,0},{1,3},{2,2},{3,1},{4,4},{5,7},{6,6},{7,5},{8,8},{9,11},{10,1... | collective-permute-start | bytes 786440 | tf_op jit(solution)/shard_map/ppermute | solution.py:27
  17.7 3.3 %collective-permute-done.5.refs_0_ = bf16[4,16,2048]{2,1,0:T(8,128)(2,1)S(1)} collective-permute-done((bf16[4,16,2048]{2,1,0:T(8,128)(2,1)S(1)}, bf16[4,16,2048]{2,1,0:T(8,128)(2,1)S(1)}, u32[]{:S(2)}, u32[]{:S(2)}) %collective-permute-start.5) | collective-permute-done | bytes 262176 | tf_op jit(solution)/shard_map/ppermute | solution.py:27
  21.0 0.6 %collective-permute-start.11 = (bf16[4,16,2048]{2,1,0:T(8,128)(2,1)S(1)}, bf16[4,16,2048]{2,1,0:T(8,128)(2,1)S(1)}, u32[]{:S(2)}, u32[]{:S(2)}) collective-permute-start(bf16[4,16,2048]{2,1,0:T(8,128)(2,1)S(1)} %collective-permute-done.5.refs_0_), channel_id=1, source_target_pairs={{0,1},{1,0},{2,3},{3,2},{4,5},{5,4},{6,7},{7,6},{8,9},{9,8},{10,11... | collective-permute-start | bytes 786440 | tf_op jit(solution)/shard_map/ppermute | solution.py:31
  21.6 2.5 %collective-permute-start.12 = (bf16[4,16,2048]{2,1,0:T(8,128)(2,1)S(1)}, bf16[4,16,2048]{2,1,0:T(8,128)(2,1)S(1)}, u32[]{:S(2)}, u32[]{:S(2)}) collective-permute-start(bf16[4,16,2048]{2,1,0:T(8,128)(2,1)S(1)} %collective-permute-done.8.refs_1_), channel_id=1, source_target_pairs={{0,1},{1,0},{2,3},{3,2},{4,5},{5,4},{6,7},{7,6},{8,9},{9,8},{10,11... | collective-permute-start | bytes 786440 | tf_op jit(solution)/shard_map/ppermute | solution.py:31
  24.1 1.3 %shard_map.80 = (f32[64,2176]{1,0:T(8,128)S(1)}, bf16[64,2176]{1,0:T(8,128)(2,1)S(1)}) custom-call(bf16[4,16,2048]{2,1,0:T(8,128)(2,1)S(1)} %collective-permute-done.2.refs_0_, bf16[4,16,2048]{2,1,0:T(8,128)(2,1)S(1)} %collective-permute-done.3.refs_1_, bf16[4,16,2048]{2,1,0:T(8,128)(2,1)S(1)} %collective-permute-done.4.refs_2_, ...), custom_call_target="tpu_custom_call" | custom-call | flops 503316480 | bytes 3407872 | tf_op jit(solution)/shard_map/pallas_call | solution.py:136
  25.5 1.3 %shard_map.81 = (f32[64,2176]{1,0:T(8,128)S(1)}, bf16[64,2176]{1,0:T(8,128)(2,1)S(1)}) custom-call(bf16[4,16,2048]{2,1,0:T(8,128)(2,1)S(1)} %collective-permute-done.5.refs_0_, bf16[4,16,2048]{2,1,0:T(8,128)(2,1)S(1)} %collective-permute-done.8.refs_1_, bf16[4,16,2048]{2,1,0:T(8,128)(2,1)S(1)} %collective-permute-done.11.refs_2_, ...), custom_call_target="tpu_custom_call" | custom-call | flops 503316480 | bytes 3407872 | tf_op jit(solution)/shard_map/pallas_call | solution.py:136
  26.8 0.6 %collective-permute-start.13 = (bf16[64,2176]{1,0:T(8,128)(2,1)S(1)}, bf16[64,2176]{1,0:T(8,128)(2,1)S(1)}, u32[]{:S(2)}, u32[]{:S(2)}) collective-permute-start(bf16[64,2176]{1,0:T(8,128)(2,1)S(1)} %get-tuple-element.25), channel_id=1, source_target_pairs={{0,1},{1,0},{2,3},{3,2},{4,5},{5,4},{6,7},{7,6},{8,9},{9,8},{10,11... | collective-permute-start | bytes 835592 | tf_op jit(solution)/shard_map/ppermute | solution.py:31
  27.5 1.6 %collective-permute-start.10 = (bf16[32,2176]{1,0:T(8,128)(2,1)S(1)}, bf16[32,2176]{1,0:T(8,128)(2,1)S(1)}, u32[]{:S(2)}, u32[]{:S(2)}) collective-permute-start(bf16[32,2176]{1,0:T(8,128)(2,1)S(1)} %get-tuple-element.27), channel_id=1, source_target_pairs={{0,2},{1,13},{2,0},{3,15},{4,6},{5,9},{6,4},{7,11},{8,10},{9,5},{1... | collective-permute-start | bytes 417800 | tf_op jit(solution)/shard_map/ppermute | solution.py:27
  29.0 2.7 %collective-permute-start.9 = (bf16[32,2176]{1,0:T(8,128)(2,1)S(1)}, bf16[32,2176]{1,0:T(8,128)(2,1)S(1)}, u32[]{:S(2)}, u32[]{:S(2)}) collective-permute-start(bf16[32,2176]{1,0:T(8,128)(2,1)S(1)} %get-tuple-element.26), channel_id=1, source_target_pairs={{0,4},{1,9},{2,6},{3,11},{4,0},{5,13},{6,2},{7,15},{8,12},{9,1},{1... | collective-permute-start | bytes 417800 | tf_op jit(solution)/shard_map/ppermute | solution.py:27
  31.8 0.5 %collective-permute-start.14 = (bf16[32,2176]{1,0:T(8,128)(2,1)S(1)}, bf16[32,2176]{1,0:T(8,128)(2,1)S(1)}, u32[]{:S(2)}, u32[]{:S(2)}) collective-permute-start(bf16[32,2176]{1,0:T(8,128)(2,1)S(1)} %get-tuple-element.28), channel_id=1, source_target_pairs={{0,6},{1,11},{2,4},{3,9},{4,2},{5,15},{6,0},{7,13},{8,14},{9,3},{1... | collective-permute-start | bytes 417800 | tf_op jit(solution)/shard_map/ppermute | solution.py:27
  32.4 0.7 %collective-permute-start.15 = (bf16[32,2176]{1,0:T(8,128)(2,1)S(1)}, bf16[32,2176]{1,0:T(8,128)(2,1)S(1)}, u32[]{:S(2)}, u32[]{:S(2)}) collective-permute-start(bf16[32,2176]{1,0:T(8,128)(2,1)S(1)} %get-tuple-element.29), channel_id=1, source_target_pairs={{0,0},{1,15},{2,2},{3,13},{4,4},{5,11},{6,6},{7,9},{8,8},{9,7},{10... | collective-permute-start | bytes 417800 | tf_op jit(solution)/shard_map/ppermute | solution.py:27
  33.1 2.8 %collective-permute-done.9 = bf16[32,2176]{1,0:T(8,128)(2,1)S(1)} collective-permute-done((bf16[32,2176]{1,0:T(8,128)(2,1)S(1)}, bf16[32,2176]{1,0:T(8,128)(2,1)S(1)}, u32[]{:S(2)}, u32[]{:S(2)}) %collective-permute-start.9) | collective-permute-done | bytes 139296 | tf_op jit(solution)/shard_map/ppermute | solution.py:27
  35.8 3.3 %collective-permute-done.14 = bf16[32,2176]{1,0:T(8,128)(2,1)S(1)} collective-permute-done((bf16[32,2176]{1,0:T(8,128)(2,1)S(1)}, bf16[32,2176]{1,0:T(8,128)(2,1)S(1)}, u32[]{:S(2)}, u32[]{:S(2)}) %collective-permute-start.14) | collective-permute-done | bytes 139296 | tf_op jit(solution)/shard_map/ppermute | solution.py:27
  39.2 4.6 %collective-permute-start.16 = (f32[16,2176]{1,0:T(8,128)S(1)}, f32[16,2176]{1,0:T(8,128)S(1)}, u32[]{:S(2)}, u32[]{:S(2)}) collective-permute-start(f32[16,2176]{1,0:T(8,128)S(1)} %slice.46), channel_id=1, source_target_pairs={{0,1},{1,0},{2,3},{3,2},{4,5},{5,4},{6,7},{7,6},{8,9},{9,8},{10,11... | collective-permute-start | bytes 417800 | tf_op jit(solution)/shard_map/ppermute | solution.py:31
  43.8 1.0 %collective-permute-done.16 = f32[16,2176]{1,0:T(8,128)S(1)} collective-permute-done((f32[16,2176]{1,0:T(8,128)S(1)}, f32[16,2176]{1,0:T(8,128)S(1)}, u32[]{:S(2)}, u32[]{:S(2)}) %collective-permute-start.16) | collective-permute-done | bytes 139296 | tf_op jit(solution)/shard_map/ppermute | solution.py:31
  44.8 1.3 %collective-permute-start.17 = (bf16[16,2048]{1,0:T(8,128)(2,1)S(1)}, bf16[16,2048]{1,0:T(8,128)(2,1)S(1)}, u32[]{:S(2)}, u32[]{:S(2)}) collective-permute-start(bf16[16,2048]{1,0:T(8,128)(2,1)S(1)} %slice.51), channel_id=1, source_target_pairs={{16,0},{17,1},{18,2},{19,3},{20,4},{21,5},{22,6},{23,7},{24,8},{25... | collective-permute-start | bytes 196616 | tf_op jit(solution)/shard_map/ppermute | solution.py:37
  46.2 0.6 %reduce_sum.9 = f32[16,2]{0,1:T(2,128)} reduce(f32[16,4,2]{0,2,1:T(2,128)S(1)} %bitcast.22, f32[]{:T(128)} %constant.0.clone.1), dimensions={1}, to_apply=%region_0.0 | reduce | flops 96 | bytes 644 | tf_op jit(solution)/shard_map/reduce_sum | solution.py:221
  46.8 4.3 %collective-permute-done.17 = bf16[16,2048]{1,0:T(8,128)(2,1)S(1)} collective-permute-done((bf16[16,2048]{1,0:T(8,128)(2,1)S(1)}, bf16[16,2048]{1,0:T(8,128)(2,1)S(1)}, u32[]{:S(2)}, u32[]{:S(2)}) %collective-permute-start.17) | collective-permute-done | bytes 65568 | tf_op jit(solution)/shard_map/ppermute | solution.py:37
  51.1 0.6 %copy.10 = bf16[1,16,2048]{2,1,0:T(8,128)(2,1)} copy(bf16[1,16,2048]{2,1,0:T(8,128)(2,1)S(1)} %bitcast.17) | data formatting | bytes 131072
  (26 shorter events, 0.5 us)
Async XLA Ops:
  0.6 1.6 %collective-permute-start = (bf16[16,2048]{1,0:T(8,128)(2,1)}, bf16[16,2048]{1,0:T(8,128)(2,1)S(1)}, u32[]{:S(2)}, u32[]{:S(2)}) collective-permute-start(bf16[16,2048]{1,0:T(8,128)(2,1)} %bitcast.18), channel_id=1, source_target_pairs={{0,1},{1,0},{2,3},{3,2},{4,5},{5,4},{6,7},{7,6},{8,9},{9,8},{10,11... | collective-permute-start | bytes 196616 | tf_op jit(solution)/shard_map/ppermute | solution.py:31
  1.1 1.5 %collective-permute-start.1 = (bf16[16,2048]{1,0:T(8,128)(2,1)}, bf16[16,2048]{1,0:T(8,128)(2,1)S(1)}, u32[]{:S(2)}, u32[]{:S(2)}) collective-permute-start(bf16[16,2048]{1,0:T(8,128)(2,1)} %bitcast.20), channel_id=1, source_target_pairs={{0,1},{1,0},{2,3},{3,2},{4,5},{5,4},{6,7},{7,6},{8,9},{9,8},{10,11... | collective-permute-start | bytes 196616 | tf_op jit(solution)/shard_map/ppermute | solution.py:31
  2.6 9.5 %collective-permute-start.2 = (bf16[4,16,2048]{2,1,0:T(8,128)(2,1)S(1)}, bf16[4,16,2048]{2,1,0:T(8,128)(2,1)S(1)}, u32[]{:S(2)}, u32[]{:S(2)}) collective-permute-start(bf16[4,16,2048]{2,1,0:T(8,128)(2,1)S(1)} %shard_map.78._.refs_4_), channel_id=1, source_target_pairs={{0,4},{1,9},{2,6},{3,11},{4,0},{5,13},{6,2},{7,15},{8,12},{9,1},{1... | collective-permute-start | bytes 786440 | tf_op jit(solution)/shard_map/ppermute | solution.py:27
  5.4 9.1 %collective-permute-start.3 = (bf16[4,16,2048]{2,1,0:T(8,128)(2,1)S(1)}, bf16[4,16,2048]{2,1,0:T(8,128)(2,1)S(1)}, u32[]{:S(2)}, u32[]{:S(2)}) collective-permute-start(bf16[4,16,2048]{2,1,0:T(8,128)(2,1)S(1)} %shard_map.78._.refs_4_), channel_id=1, source_target_pairs={{0,2},{1,13},{2,0},{3,15},{4,6},{5,9},{6,4},{7,11},{8,10},{9,5},{1... | collective-permute-start | bytes 786440 | tf_op jit(solution)/shard_map/ppermute | solution.py:27
  6.9 0.7 %copy-start = (s32[1,256,2]{1,2,0:T(2,128)S(1)}, s32[1,256,2]{1,2,0:T(2,128)}, u32[]{:S(2)}) copy-start(s32[1,256,2]{1,2,0:T(2,128)} %param.8) | copy-start | bytes 6148
  7.6 0.7 %copy-start.1 = (bf16[1,256,2]{1,2,0:T(2,128)(2,1)S(1)}, bf16[1,256,2]{1,2,0:T(2,128)(2,1)}, u32[]{:S(2)}) copy-start(bf16[1,256,2]{1,2,0:T(2,128)(2,1)} %param.9) | copy-start | bytes 3076
  12.2 8.8 %collective-permute-start.5 = (bf16[4,16,2048]{2,1,0:T(8,128)(2,1)S(1)}, bf16[4,16,2048]{2,1,0:T(8,128)(2,1)S(1)}, u32[]{:S(2)}, u32[]{:S(2)}) collective-permute-start(bf16[4,16,2048]{2,1,0:T(8,128)(2,1)S(1)} %collective-permute-done.2.refs_0_), channel_id=1, source_target_pairs={{0,2},{1,3},{2,0},{3,1},{4,6},{5,7},{6,4},{7,5},{8,10},{9,11},{10,... | collective-permute-start | bytes 786440 | tf_op jit(solution)/shard_map/ppermute | solution.py:27
  14.5 9.6 %collective-permute-start.4 = (bf16[4,16,2048]{2,1,0:T(8,128)(2,1)S(1)}, bf16[4,16,2048]{2,1,0:T(8,128)(2,1)S(1)}, u32[]{:S(2)}, u32[]{:S(2)}) collective-permute-start(bf16[4,16,2048]{2,1,0:T(8,128)(2,1)S(1)} %collective-permute-done.2.refs_0_), channel_id=1, source_target_pairs={{0,1},{1,0},{2,3},{3,2},{4,5},{5,4},{6,7},{7,6},{8,9},{9,8},{10,11... | collective-permute-start | bytes 786440 | tf_op jit(solution)/shard_map/ppermute | solution.py:31
  17.0 4.6 %collective-permute-start.8 = (bf16[4,16,2048]{2,1,0:T(8,128)(2,1)S(1)}, bf16[4,16,2048]{2,1,0:T(8,128)(2,1)S(1)}, u32[]{:S(2)}, u32[]{:S(2)}) collective-permute-start(bf16[4,16,2048]{2,1,0:T(8,128)(2,1)S(1)} %collective-permute-done.3.refs_1_), channel_id=1, source_target_pairs={{0,0},{1,3},{2,2},{3,1},{4,4},{5,7},{6,6},{7,5},{8,8},{9,11},{10,1... | collective-permute-start | bytes 786440 | tf_op jit(solution)/shard_map/ppermute | solution.py:27
  21.0 3.1 %collective-permute-start.6 = (bf16[4,16,2048]{2,1,0:T(8,128)(2,1)S(1)}, bf16[4,16,2048]{2,1,0:T(8,128)(2,1)S(1)}, u32[]{:S(2)}, u32[]{:S(2)}) collective-permute-start(bf16[4,16,2048]{2,1,0:T(8,128)(2,1)S(1)} %collective-permute-done.3.refs_1_), channel_id=1, source_target_pairs={{0,1},{1,0},{2,3},{3,2},{4,5},{5,4},{6,7},{7,6},{8,9},{9,8},{10,11... | collective-permute-start | bytes 786440 | tf_op jit(solution)/shard_map/ppermute | solution.py:31
  21.0 4.5 %collective-permute-start.11 = (bf16[4,16,2048]{2,1,0:T(8,128)(2,1)S(1)}, bf16[4,16,2048]{2,1,0:T(8,128)(2,1)S(1)}, u32[]{:S(2)}, u32[]{:S(2)}) collective-permute-start(bf16[4,16,2048]{2,1,0:T(8,128)(2,1)S(1)} %collective-permute-done.5.refs_0_), channel_id=1, source_target_pairs={{0,1},{1,0},{2,3},{3,2},{4,5},{5,4},{6,7},{7,6},{8,9},{9,8},{10,11... | collective-permute-start | bytes 786440 | tf_op jit(solution)/shard_map/ppermute | solution.py:31
  21.6 3.9 %collective-permute-start.12 = (bf16[4,16,2048]{2,1,0:T(8,128)(2,1)S(1)}, bf16[4,16,2048]{2,1,0:T(8,128)(2,1)S(1)}, u32[]{:S(2)}, u32[]{:S(2)}) collective-permute-start(bf16[4,16,2048]{2,1,0:T(8,128)(2,1)S(1)} %collective-permute-done.8.refs_1_), channel_id=1, source_target_pairs={{0,1},{1,0},{2,3},{3,2},{4,5},{5,4},{6,7},{7,6},{8,9},{9,8},{10,11... | collective-permute-start | bytes 786440 | tf_op jit(solution)/shard_map/ppermute | solution.py:31
  25.4 1.9 %collective-permute-start.7 = (bf16[64,2176]{1,0:T(8,128)(2,1)S(1)}, bf16[64,2176]{1,0:T(8,128)(2,1)S(1)}, u32[]{:S(2)}, u32[]{:S(2)}) collective-permute-start(bf16[64,2176]{1,0:T(8,128)(2,1)S(1)} %get-tuple-element.22), channel_id=1, source_target_pairs={{0,1},{1,0},{2,3},{3,2},{4,5},{5,4},{6,7},{7,6},{8,9},{9,8},{10,11... | collective-permute-start | bytes 835592 | tf_op jit(solution)/shard_map/ppermute | solution.py:31
  26.8 4.9 %collective-permute-start.13 = (bf16[64,2176]{1,0:T(8,128)(2,1)S(1)}, bf16[64,2176]{1,0:T(8,128)(2,1)S(1)}, u32[]{:S(2)}, u32[]{:S(2)}) collective-permute-start(bf16[64,2176]{1,0:T(8,128)(2,1)S(1)} %get-tuple-element.25), channel_id=1, source_target_pairs={{0,1},{1,0},{2,3},{3,2},{4,5},{5,4},{6,7},{7,6},{8,9},{9,8},{10,11... | collective-permute-start | bytes 835592 | tf_op jit(solution)/shard_map/ppermute | solution.py:31
  27.5 5.6 %collective-permute-start.10 = (bf16[32,2176]{1,0:T(8,128)(2,1)S(1)}, bf16[32,2176]{1,0:T(8,128)(2,1)S(1)}, u32[]{:S(2)}, u32[]{:S(2)}) collective-permute-start(bf16[32,2176]{1,0:T(8,128)(2,1)S(1)} %get-tuple-element.27), channel_id=1, source_target_pairs={{0,2},{1,13},{2,0},{3,15},{4,6},{5,9},{6,4},{7,11},{8,10},{9,5},{1... | collective-permute-start | bytes 417800 | tf_op jit(solution)/shard_map/ppermute | solution.py:27
  29.0 6.8 %collective-permute-start.9 = (bf16[32,2176]{1,0:T(8,128)(2,1)S(1)}, bf16[32,2176]{1,0:T(8,128)(2,1)S(1)}, u32[]{:S(2)}, u32[]{:S(2)}) collective-permute-start(bf16[32,2176]{1,0:T(8,128)(2,1)S(1)} %get-tuple-element.26), channel_id=1, source_target_pairs={{0,4},{1,9},{2,6},{3,11},{4,0},{5,13},{6,2},{7,15},{8,12},{9,1},{1... | collective-permute-start | bytes 417800 | tf_op jit(solution)/shard_map/ppermute | solution.py:27
  31.8 7.2 %collective-permute-start.14 = (bf16[32,2176]{1,0:T(8,128)(2,1)S(1)}, bf16[32,2176]{1,0:T(8,128)(2,1)S(1)}, u32[]{:S(2)}, u32[]{:S(2)}) collective-permute-start(bf16[32,2176]{1,0:T(8,128)(2,1)S(1)} %get-tuple-element.28), channel_id=1, source_target_pairs={{0,6},{1,11},{2,4},{3,9},{4,2},{5,15},{6,0},{7,13},{8,14},{9,3},{1... | collective-permute-start | bytes 417800 | tf_op jit(solution)/shard_map/ppermute | solution.py:27
  32.4 6.7 %collective-permute-start.15 = (bf16[32,2176]{1,0:T(8,128)(2,1)S(1)}, bf16[32,2176]{1,0:T(8,128)(2,1)S(1)}, u32[]{:S(2)}, u32[]{:S(2)}) collective-permute-start(bf16[32,2176]{1,0:T(8,128)(2,1)S(1)} %get-tuple-element.29), channel_id=1, source_target_pairs={{0,0},{1,15},{2,2},{3,13},{4,4},{5,11},{6,6},{7,9},{8,8},{9,7},{10... | collective-permute-start | bytes 417800 | tf_op jit(solution)/shard_map/ppermute | solution.py:27
  39.2 5.6 %collective-permute-start.16 = (f32[16,2176]{1,0:T(8,128)S(1)}, f32[16,2176]{1,0:T(8,128)S(1)}, u32[]{:S(2)}, u32[]{:S(2)}) collective-permute-start(f32[16,2176]{1,0:T(8,128)S(1)} %slice.46), channel_id=1, source_target_pairs={{0,1},{1,0},{2,3},{3,2},{4,5},{5,4},{6,7},{7,6},{8,9},{9,8},{10,11... | collective-permute-start | bytes 417800 | tf_op jit(solution)/shard_map/ppermute | solution.py:31
  44.8 6.3 %collective-permute-start.17 = (bf16[16,2048]{1,0:T(8,128)(2,1)S(1)}, bf16[16,2048]{1,0:T(8,128)(2,1)S(1)}, u32[]{:S(2)}, u32[]{:S(2)}) collective-permute-start(bf16[16,2048]{1,0:T(8,128)(2,1)S(1)} %slice.51), channel_id=1, source_target_pairs={{16,0},{17,1},{18,2},{19,3},{20,4},{21,5},{22,6},{23,7},{24,8},{25... | collective-permute-start | bytes 196616 | tf_op jit(solution)/shard_map/ppermute | solution.py:37

commit v4 on v3

--- a/solution.py
+++ b/solution.py
@@ -200,19 +200,18 @@
     )(expert_ids[0].T, gate_weights[0].T, in_hbm(gate_up), in_hbm(down_mat), chip)
 
     first = [exchange(chip, *slots[k]) for k in range(half)]
-    first[0] = after(first[0], aux)
+    first[-1] = after(first[-1], aux)
     then = [exchange(first[k], (0, 1), (0, 1) if k < half - 1 else (0, 0)) for k in range(half)]
-    swapped = [swap(after(value, first[-1])) for value in first[:-1]] + [swap(after(first[-1], then[0]))]
+    swapped = [swap(after(value, first[-1])) for value in first[:-1]] + [swap(first[-1])]
     near = size * rows // 2
-    keep, send1 = expert_grads(first + swapped, [], aux[:near], weights)
+    keep, send1 = expert_grads(first + swapped, [], after(aux[:near], then[0]), weights)
     came = after(swap(send1), then[-1])
     total1 = (keep + came.astype(jnp.float32)).astype(jnp.bfloat16)
-    late = [value for value in then[:-1]]
-    late.append(then[-1])
-    swapped = [swap(value) for value in late]
-    keep, send = expert_grads(late + swapped, [chip], aux[near:], weights)
-    total = (keep + swap(send).astype(jnp.float32)).astype(jnp.bfloat16)
     received = [exchange(total1[k * 2 * rows:(k + 1) * 2 * rows], *slots[k]) for k in range(half)]
+    swapped = [swap(value) for value in then]
+    keep, send = expert_grads(then + swapped, [chip], aux[near:], weights)
+    came = after(swap(send), total1)
+    total = (keep + came.astype(jnp.float32)).astype(jnp.bfloat16)
     received += [exchange(total[k * 2 * rows:(k + 1) * 2 * rows], *slots[half + k]) for k in range(half)]
     total = sum(part.astype(jnp.float32) for part in received)
     final = total[:rows] + swap(total[rows:])

time: 52 us -> 52 us (level)
  waiting for transfers between devices: 16.7 us -> 14 us
  starting transfers between devices: 25.5 us -> 28.1 us
    ppermute x8, waiting for transfers between devices: 10.9 us -> 8.24 us  [exchange(): return lax.ppermute(value, 'expert', pairs)]
    ppermute x9, starting transfers between devices: 11.4 us -> 14 us  [swap(): lax.ppermute(value, 'expert', [(i, i ^ 1) for i in range(lax.axis_size('e...]
where the time goes in v4:
time: 52 us; the launch traced here: 51.7 us
  starting transfers between devices  28.1 us (54%)
  waiting for transfers between devices  14 us (27%)
  Pallas kernels  5.86 us (11%)
  local copies, waits for them, and re-layouts  2.13 us (4%)
  other arithmetic  0.78 us (2%)
  between operations  0.78 us (2%)
    ppermute x9, starting transfers between devices, swap(): lax.ppermute(value, 'expert', [(i, i ^ 1) for i in range(lax.axis_size('e...  14 us
    ppermute x8, starting transfers between devices, exchange(): return lax.ppermute(value, 'expert', pairs)  12.8 us
    ppermute x8, waiting for transfers between devices, exchange(): return lax.ppermute(value, 'expert', pairs)  8.24 us
    ppermute x1, waiting for transfers between devices, from_behind(): return lax.ppermute(shard, axis, pairs)  4.29 us
    pallas_call x2, Pallas kernels, expert_grads(): pl.pallas_call(functools.partial(grads_kernel, len(blocks), bool(own)), o...  2.57 us
    pallas_call x1, Pallas kernels, body(): pl.pallas_call(functools.partial(stage_kernel, planes, rows), in_specs=[h...  2.38 us
    unnamed x5, local copies, waits for them, and re-layouts  1.99 us
    ppermute x9, waiting for transfers between devices, swap(): lax.ppermute(value, 'expert', [(i, i ^ 1) for i in range(lax.axis_size('e...  1.5 us
  transfers between devices with their start and end apart: 18, of which 8 were waited for; matrix products, arithmetic and copies ran while one was open for 2% of the time, Pallas kernels for 11%

profile of v4, /device:TPU:0, one launch (start us, length us, event | category | flops | bytes accessed | tf_op | source)
XLA Modules:
  0.0 51.7 jit_solution(5035136148248981637)
XLA Ops:
  0.6 0.5 %collective-permute-start = (bf16[16,2048]{1,0:T(8,128)(2,1)}, bf16[16,2048]{1,0:T(8,128)(2,1)S(1)}, u32[]{:S(2)}, u32[]{:S(2)}) collective-permute-start(bf16[16,2048]{1,0:T(8,128)(2,1)} %bitcast.18), channel_id=1, source_target_pairs={{0,1},{1,0},{2,3},{3,2},{4,5},{5,4},{6,7},{7,6},{8,9},{9,8},{10,11... | collective-permute-start | bytes 196616 | tf_op jit(solution)/shard_map/ppermute | solution.py:31
  1.2 0.9 %shard_map.77.own_ref = bf16[2,16,2048]{2,1,0:T(8,128)(2,1)S(1)} custom-call(bf16[16,2048]{1,0:T(8,128)(2,1)} %bitcast.19, bf16[16,2048]{1,0:T(8,128)(2,1)} %bitcast.21), custom_call_target="tpu_custom_call" | custom-call | tf_op jit(solution)/shard_map/pallas_call | solution.py:166
  2.1 0.1 collective-permute-done.a_ref
  2.3 0.4 collective-permute-done.1.b_ref
  2.6 2.8 %collective-permute-start.2 = (bf16[4,16,2048]{2,1,0:T(8,128)(2,1)S(1)}, bf16[4,16,2048]{2,1,0:T(8,128)(2,1)S(1)}, u32[]{:S(2)}, u32[]{:S(2)}) collective-permute-start(bf16[4,16,2048]{2,1,0:T(8,128)(2,1)S(1)} %shard_map.78._.refs_4_), channel_id=1, source_target_pairs={{0,4},{1,9},{2,6},{3,11},{4,0},{5,13},{6,2},{7,15},{8,12},{9,1},{1... | collective-permute-start | bytes 786440 | tf_op jit(solution)/shard_map/ppermute | solution.py:27
  5.4 1.5 %collective-permute-start.3 = (bf16[4,16,2048]{2,1,0:T(8,128)(2,1)S(1)}, bf16[4,16,2048]{2,1,0:T(8,128)(2,1)S(1)}, u32[]{:S(2)}, u32[]{:S(2)}) collective-permute-start(bf16[4,16,2048]{2,1,0:T(8,128)(2,1)S(1)} %shard_map.78._.refs_4_), channel_id=1, source_target_pairs={{0,2},{1,13},{2,0},{3,15},{4,6},{5,9},{6,4},{7,11},{8,10},{9,5},{1... | collective-permute-start | bytes 786440 | tf_op jit(solution)/shard_map/ppermute | solution.py:27
  7.0 0.7 %copy-done = s32[1,256,2]{1,2,0:T(2,128)S(1)} copy-done((s32[1,256,2]{1,2,0:T(2,128)S(1)}, s32[1,256,2]{1,2,0:T(2,128)}, u32[]{:S(2)}) %copy-start) | copy-done | bytes 2072
  7.6 0.7 %copy-done.1 = bf16[1,256,2]{1,2,0:T(2,128)(2,1)S(1)} copy-done((bf16[1,256,2]{1,2,0:T(2,128)(2,1)S(1)}, bf16[1,256,2]{1,2,0:T(2,128)(2,1)}, u32[]{:S(2)}) %copy-start.1) | copy-done | bytes 1048
  8.3 2.4 %shard_map.79 = (f32[256,8]{1,0:T(8,128)S(1)}, bf16[384,2048]{1,0:T(8,128)(2,1)S(1)}, bf16[2048,384]{1,0:T(8,128)(2,1)S(1)}, bf16[2048,192]{1,0:T(8,128)(2,1)S(1)}) custom-call(s32[2,256]{1,0:T(2,128)S(1)} %bitcast.13, bf16[2,256]{1,0:T(2,128)(2,1)S(1)} %bitcast.14, bf16[384,2048]{1,0:T(8,128)(2,1)} %bitcast.15, bf16[192,2048]{1,0:T(8,128)(2,1)} %bitcast.16, ...), custom_call_target="tpu_custom_call" | custom-call | bytes 4718592 | tf_op jit(solution)/shard_map/pallas_call | solution.py:181
  10.7 1.5 %collective-permute-done.2.refs_0_ = bf16[4,16,2048]{2,1,0:T(8,128)(2,1)S(1)} collective-permute-done((bf16[4,16,2048]{2,1,0:T(8,128)(2,1)S(1)}, bf16[4,16,2048]{2,1,0:T(8,128)(2,1)S(1)}, u32[]{:S(2)}, u32[]{:S(2)}) %collective-permute-start.2) | collective-permute-done | bytes 262176 | tf_op jit(solution)/shard_map/ppermute | solution.py:27
  12.2 2.3 %collective-permute-start.6 = (bf16[4,16,2048]{2,1,0:T(8,128)(2,1)S(1)}, bf16[4,16,2048]{2,1,0:T(8,128)(2,1)S(1)}, u32[]{:S(2)}, u32[]{:S(2)}) collective-permute-start(bf16[4,16,2048]{2,1,0:T(8,128)(2,1)S(1)} %collective-permute-done.2.refs_0_), channel_id=1, source_target_pairs={{0,2},{1,3},{2,0},{3,1},{4,6},{5,7},{6,4},{7,5},{8,10},{9,11},{10,... | collective-permute-start | bytes 786440 | tf_op jit(solution)/shard_map/ppermute | solution.py:27
  14.5 0.7 %collective-permute-start.8 = (bf16[4,16,2048]{2,1,0:T(8,128)(2,1)S(1)}, bf16[4,16,2048]{2,1,0:T(8,128)(2,1)S(1)}, u32[]{:S(2)}, u32[]{:S(2)}) collective-permute-start(bf16[4,16,2048]{2,1,0:T(8,128)(2,1)S(1)} %collective-permute-done.3.refs_1_), channel_id=1, source_target_pairs={{0,0},{1,3},{2,2},{3,1},{4,4},{5,7},{6,6},{7,5},{8,8},{9,11},{10,1... | collective-permute-start | bytes 786440 | tf_op jit(solution)/shard_map/ppermute | solution.py:27
  15.2 5.1 %collective-permute-start.4 = (bf16[4,16,2048]{2,1,0:T(8,128)(2,1)S(1)}, bf16[4,16,2048]{2,1,0:T(8,128)(2,1)S(1)}, u32[]{:S(2)}, u32[]{:S(2)}) collective-permute-start(bf16[4,16,2048]{2,1,0:T(8,128)(2,1)S(1)} %collective-permute-done.2.refs_0_), channel_id=1, source_target_pairs={{0,1},{1,0},{2,3},{3,2},{4,5},{5,4},{6,7},{7,6},{8,9},{9,8},{10,11... | collective-permute-start | bytes 786440 | tf_op jit(solution)/shard_map/ppermute | solution.py:31
  20.2 0.1 collective-permute-start.5
  20.3 0.7 %collective-permute-done.6.refs_0_ = bf16[4,16,2048]{2,1,0:T(8,128)(2,1)S(1)} collective-permute-done((bf16[4,16,2048]{2,1,0:T(8,128)(2,1)S(1)}, bf16[4,16,2048]{2,1,0:T(8,128)(2,1)S(1)}, u32[]{:S(2)}, u32[]{:S(2)}) %collective-permute-start.6) | collective-permute-done | bytes 262176 | tf_op jit(solution)/shard_map/ppermute | solution.py:27
  21.0 3.1 %collective-permute-start.12 = (bf16[4,16,2048]{2,1,0:T(8,128)(2,1)S(1)}, bf16[4,16,2048]{2,1,0:T(8,128)(2,1)S(1)}, u32[]{:S(2)}, u32[]{:S(2)}) collective-permute-start(bf16[4,16,2048]{2,1,0:T(8,128)(2,1)S(1)} %collective-permute-done.8.refs_1_), channel_id=1, source_target_pairs={{0,1},{1,0},{2,3},{3,2},{4,5},{5,4},{6,7},{7,6},{8,9},{9,8},{10,11... | collective-permute-start | bytes 786440 | tf_op jit(solution)/shard_map/ppermute | solution.py:31
  24.1 1.3 %shard_map.80 = (f32[64,2176]{1,0:T(8,128)S(1)}, bf16[64,2176]{1,0:T(8,128)(2,1)S(1)}) custom-call(bf16[4,16,2048]{2,1,0:T(8,128)(2,1)S(1)} %collective-permute-done.2.refs_0_, bf16[4,16,2048]{2,1,0:T(8,128)(2,1)S(1)} %collective-permute-done.3.refs_1_, bf16[4,16,2048]{2,1,0:T(8,128)(2,1)S(1)} %collective-permute-done.4.refs_2_, ...), custom_call_target="tpu_custom_call" | custom-call | flops 503316480 | bytes 3407872 | tf_op jit(solution)/shard_map/pallas_call | solution.py:136
  25.4 0.1 collective-permute-start.7
  25.5 1.3 %shard_map.81 = (f32[64,2176]{1,0:T(8,128)S(1)}, bf16[64,2176]{1,0:T(8,128)(2,1)S(1)}) custom-call(bf16[4,16,2048]{2,1,0:T(8,128)(2,1)S(1)} %collective-permute-done.6.refs_0_, bf16[4,16,2048]{2,1,0:T(8,128)(2,1)S(1)} %collective-permute-done.8.refs_1_, bf16[4,16,2048]{2,1,0:T(8,128)(2,1)S(1)} %collective-permute-done.11.refs_2_, ...), custom_call_target="tpu_custom_call" | custom-call | flops 503316480 | bytes 3407872 | tf_op jit(solution)/shard_map/pallas_call | solution.py:136
  26.8 0.5 %collective-permute-start.13 = (bf16[64,2176]{1,0:T(8,128)(2,1)S(1)}, bf16[64,2176]{1,0:T(8,128)(2,1)S(1)}, u32[]{:S(2)}, u32[]{:S(2)}) collective-permute-start(bf16[64,2176]{1,0:T(8,128)(2,1)S(1)} %get-tuple-element.26), channel_id=1, source_target_pairs={{0,1},{1,0},{2,3},{3,2},{4,5},{5,4},{6,7},{7,6},{8,9},{9,8},{10,11... | collective-permute-start | bytes 835592 | tf_op jit(solution)/shard_map/ppermute | solution.py:31
  27.4 1.6 %collective-permute-start.10 = (bf16[32,2176]{1,0:T(8,128)(2,1)S(1)}, bf16[32,2176]{1,0:T(8,128)(2,1)S(1)}, u32[]{:S(2)}, u32[]{:S(2)}) collective-permute-start(bf16[32,2176]{1,0:T(8,128)(2,1)S(1)} %get-tuple-element.29), channel_id=1, source_target_pairs={{0,2},{1,13},{2,0},{3,15},{4,6},{5,9},{6,4},{7,11},{8,10},{9,5},{1... | collective-permute-start | bytes 417800 | tf_op jit(solution)/shard_map/ppermute | solution.py:27
  29.0 2.7 %collective-permute-start.9 = (bf16[32,2176]{1,0:T(8,128)(2,1)S(1)}, bf16[32,2176]{1,0:T(8,128)(2,1)S(1)}, u32[]{:S(2)}, u32[]{:S(2)}) collective-permute-start(bf16[32,2176]{1,0:T(8,128)(2,1)S(1)} %get-tuple-element.28), channel_id=1, source_target_pairs={{0,4},{1,9},{2,6},{3,11},{4,0},{5,13},{6,2},{7,15},{8,12},{9,1},{1... | collective-permute-start | bytes 417800 | tf_op jit(solution)/shard_map/ppermute | solution.py:27
  31.8 0.5 %collective-permute-start.14 = (bf16[32,2176]{1,0:T(8,128)(2,1)S(1)}, bf16[32,2176]{1,0:T(8,128)(2,1)S(1)}, u32[]{:S(2)}, u32[]{:S(2)}) collective-permute-start(bf16[32,2176]{1,0:T(8,128)(2,1)S(1)} %get-tuple-element.30), channel_id=1, source_target_pairs={{0,6},{1,11},{2,4},{3,9},{4,2},{5,15},{6,0},{7,13},{8,14},{9,3},{1... | collective-permute-start | bytes 417800 | tf_op jit(solution)/shard_map/ppermute | solution.py:27
  32.4 0.7 %collective-permute-start.15 = (bf16[32,2176]{1,0:T(8,128)(2,1)S(1)}, bf16[32,2176]{1,0:T(8,128)(2,1)S(1)}, u32[]{:S(2)}, u32[]{:S(2)}) collective-permute-start(bf16[32,2176]{1,0:T(8,128)(2,1)S(1)} %get-tuple-element.31), channel_id=1, source_target_pairs={{0,0},{1,15},{2,2},{3,13},{4,4},{5,11},{6,6},{7,9},{8,8},{9,7},{10... | collective-permute-start | bytes 417800 | tf_op jit(solution)/shard_map/ppermute | solution.py:27
  33.1 2.8 %collective-permute-done.9 = bf16[32,2176]{1,0:T(8,128)(2,1)S(1)} collective-permute-done((bf16[32,2176]{1,0:T(8,128)(2,1)S(1)}, bf16[32,2176]{1,0:T(8,128)(2,1)S(1)}, u32[]{:S(2)}, u32[]{:S(2)}) %collective-permute-start.9) | collective-permute-done | bytes 139296 | tf_op jit(solution)/shard_map/ppermute | solution.py:27
  35.8 3.3 %collective-permute-done.14 = bf16[32,2176]{1,0:T(8,128)(2,1)S(1)} collective-permute-done((bf16[32,2176]{1,0:T(8,128)(2,1)S(1)}, bf16[32,2176]{1,0:T(8,128)(2,1)S(1)}, u32[]{:S(2)}, u32[]{:S(2)}) %collective-permute-start.14) | collective-permute-done | bytes 139296 | tf_op jit(solution)/shard_map/ppermute | solution.py:27
  39.2 4.6 %collective-permute-start.16 = (f32[16,2176]{1,0:T(8,128)S(1)}, f32[16,2176]{1,0:T(8,128)S(1)}, u32[]{:S(2)}, u32[]{:S(2)}) collective-permute-start(f32[16,2176]{1,0:T(8,128)S(1)} %slice.46), channel_id=1, source_target_pairs={{0,1},{1,0},{2,3},{3,2},{4,5},{5,4},{6,7},{7,6},{8,9},{9,8},{10,11... | collective-permute-start | bytes 417800 | tf_op jit(solution)/shard_map/ppermute | solution.py:31
  43.8 1.0 %collective-permute-done.16 = f32[16,2176]{1,0:T(8,128)S(1)} collective-permute-done((f32[16,2176]{1,0:T(8,128)S(1)}, f32[16,2176]{1,0:T(8,128)S(1)}, u32[]{:S(2)}, u32[]{:S(2)}) %collective-permute-start.16) | collective-permute-done | bytes 139296 | tf_op jit(solution)/shard_map/ppermute | solution.py:31
  44.8 1.3 %collective-permute-start.17 = (bf16[16,2048]{1,0:T(8,128)(2,1)S(1)}, bf16[16,2048]{1,0:T(8,128)(2,1)S(1)}, u32[]{:S(2)}, u32[]{:S(2)}) collective-permute-start(bf16[16,2048]{1,0:T(8,128)(2,1)S(1)} %slice.51), channel_id=1, source_target_pairs={{16,0},{17,1},{18,2},{19,3},{20,4},{21,5},{22,6},{23,7},{24,8},{25... | collective-permute-start | bytes 196616 | tf_op jit(solution)/shard_map/ppermute | solution.py:37
  46.2 0.6 %reduce_sum.9 = f32[16,2]{0,1:T(2,128)} reduce(f32[16,4,2]{0,2,1:T(2,128)S(1)} %bitcast.22, f32[]{:T(128)} %constant.0.clone.1), dimensions={1}, to_apply=%region_0.0 | reduce | flops 96 | bytes 644 | tf_op jit(solution)/shard_map/reduce_sum | solution.py:220
  46.8 4.3 %collective-permute-done.17 = bf16[16,2048]{1,0:T(8,128)(2,1)S(1)} collective-permute-done((bf16[16,2048]{1,0:T(8,128)(2,1)S(1)}, bf16[16,2048]{1,0:T(8,128)(2,1)S(1)}, u32[]{:S(2)}, u32[]{:S(2)}) %collective-permute-start.17) | collective-permute-done | bytes 65568 | tf_op jit(solution)/shard_map/ppermute | solution.py:37
  51.1 0.6 %copy.10 = bf16[1,16,2048]{2,1,0:T(8,128)(2,1)} copy(bf16[1,16,2048]{2,1,0:T(8,128)(2,1)S(1)} %bitcast.17) | data formatting | bytes 131072
  (26 shorter events, 0.5 us)
Async XLA Ops:
  0.6 1.6 %collective-permute-start = (bf16[16,2048]{1,0:T(8,128)(2,1)}, bf16[16,2048]{1,0:T(8,128)(2,1)S(1)}, u32[]{:S(2)}, u32[]{:S(2)}) collective-permute-start(bf16[16,2048]{1,0:T(8,128)(2,1)} %bitcast.18), channel_id=1, source_target_pairs={{0,1},{1,0},{2,3},{3,2},{4,5},{5,4},{6,7},{7,6},{8,9},{9,8},{10,11... | collective-permute-start | bytes 196616 | tf_op jit(solution)/shard_map/ppermute | solution.py:31
  1.1 1.5 %collective-permute-start.1 = (bf16[16,2048]{1,0:T(8,128)(2,1)}, bf16[16,2048]{1,0:T(8,128)(2,1)S(1)}, u32[]{:S(2)}, u32[]{:S(2)}) collective-permute-start(bf16[16,2048]{1,0:T(8,128)(2,1)} %bitcast.20), channel_id=1, source_target_pairs={{0,1},{1,0},{2,3},{3,2},{4,5},{5,4},{6,7},{7,6},{8,9},{9,8},{10,11... | collective-permute-start | bytes 196616 | tf_op jit(solution)/shard_map/ppermute | solution.py:31
  2.6 9.5 %collective-permute-start.2 = (bf16[4,16,2048]{2,1,0:T(8,128)(2,1)S(1)}, bf16[4,16,2048]{2,1,0:T(8,128)(2,1)S(1)}, u32[]{:S(2)}, u32[]{:S(2)}) collective-permute-start(bf16[4,16,2048]{2,1,0:T(8,128)(2,1)S(1)} %shard_map.78._.refs_4_), channel_id=1, source_target_pairs={{0,4},{1,9},{2,6},{3,11},{4,0},{5,13},{6,2},{7,15},{8,12},{9,1},{1... | collective-permute-start | bytes 786440 | tf_op jit(solution)/shard_map/ppermute | solution.py:27
  5.4 9.1 %collective-permute-start.3 = (bf16[4,16,2048]{2,1,0:T(8,128)(2,1)S(1)}, bf16[4,16,2048]{2,1,0:T(8,128)(2,1)S(1)}, u32[]{:S(2)}, u32[]{:S(2)}) collective-permute-start(bf16[4,16,2048]{2,1,0:T(8,128)(2,1)S(1)} %shard_map.78._.refs_4_), channel_id=1, source_target_pairs={{0,2},{1,13},{2,0},{3,15},{4,6},{5,9},{6,4},{7,11},{8,10},{9,5},{1... | collective-permute-start | bytes 786440 | tf_op jit(solution)/shard_map/ppermute | solution.py:27
  6.9 0.7 %copy-start = (s32[1,256,2]{1,2,0:T(2,128)S(1)}, s32[1,256,2]{1,2,0:T(2,128)}, u32[]{:S(2)}) copy-start(s32[1,256,2]{1,2,0:T(2,128)} %param.8) | copy-start | bytes 6148
  7.6 0.7 %copy-start.1 = (bf16[1,256,2]{1,2,0:T(2,128)(2,1)S(1)}, bf16[1,256,2]{1,2,0:T(2,128)(2,1)}, u32[]{:S(2)}) copy-start(bf16[1,256,2]{1,2,0:T(2,128)(2,1)} %param.9) | copy-start | bytes 3076
  12.2 8.8 %collective-permute-start.6 = (bf16[4,16,2048]{2,1,0:T(8,128)(2,1)S(1)}, bf16[4,16,2048]{2,1,0:T(8,128)(2,1)S(1)}, u32[]{:S(2)}, u32[]{:S(2)}) collective-permute-start(bf16[4,16,2048]{2,1,0:T(8,128)(2,1)S(1)} %collective-permute-done.2.refs_0_), channel_id=1, source_target_pairs={{0,2},{1,3},{2,0},{3,1},{4,6},{5,7},{6,4},{7,5},{8,10},{9,11},{10,... | collective-permute-start | bytes 786440 | tf_op jit(solution)/shard_map/ppermute | solution.py:27
  14.5 6.5 %collective-permute-start.8 = (bf16[4,16,2048]{2,1,0:T(8,128)(2,1)S(1)}, bf16[4,16,2048]{2,1,0:T(8,128)(2,1)S(1)}, u32[]{:S(2)}, u32[]{:S(2)}) collective-permute-start(bf16[4,16,2048]{2,1,0:T(8,128)(2,1)S(1)} %collective-permute-done.3.refs_1_), channel_id=1, source_target_pairs={{0,0},{1,3},{2,2},{3,1},{4,4},{5,7},{6,6},{7,5},{8,8},{9,11},{10,1... | collective-permute-start | bytes 786440 | tf_op jit(solution)/shard_map/ppermute | solution.py:27
  15.2 8.9 %collective-permute-start.4 = (bf16[4,16,2048]{2,1,0:T(8,128)(2,1)S(1)}, bf16[4,16,2048]{2,1,0:T(8,128)(2,1)S(1)}, u32[]{:S(2)}, u32[]{:S(2)}) collective-permute-start(bf16[4,16,2048]{2,1,0:T(8,128)(2,1)S(1)} %collective-permute-done.2.refs_0_), channel_id=1, source_target_pairs={{0,1},{1,0},{2,3},{3,2},{4,5},{5,4},{6,7},{7,6},{8,9},{9,8},{10,11... | collective-permute-start | bytes 786440 | tf_op jit(solution)/shard_map/ppermute | solution.py:31
  20.2 3.9 %collective-permute-start.5 = (bf16[4,16,2048]{2,1,0:T(8,128)(2,1)S(1)}, bf16[4,16,2048]{2,1,0:T(8,128)(2,1)S(1)}, u32[]{:S(2)}, u32[]{:S(2)}) collective-permute-start(bf16[4,16,2048]{2,1,0:T(8,128)(2,1)S(1)} %collective-permute-done.3.refs_1_), channel_id=1, source_target_pairs={{0,1},{1,0},{2,3},{3,2},{4,5},{5,4},{6,7},{7,6},{8,9},{9,8},{10,11... | collective-permute-start | bytes 786440 | tf_op jit(solution)/shard_map/ppermute | solution.py:31
  21.0 4.5 %collective-permute-start.11 = (bf16[4,16,2048]{2,1,0:T(8,128)(2,1)S(1)}, bf16[4,16,2048]{2,1,0:T(8,128)(2,1)S(1)}, u32[]{:S(2)}, u32[]{:S(2)}) collective-permute-start(bf16[4,16,2048]{2,1,0:T(8,128)(2,1)S(1)} %collective-permute-done.6.refs_0_), channel_id=1, source_target_pairs={{0,1},{1,0},{2,3},{3,2},{4,5},{5,4},{6,7},{7,6},{8,9},{9,8},{10,11... | collective-permute-start | bytes 786440 | tf_op jit(solution)/shard_map/ppermute | solution.py:31
  21.0 4.5 %collective-permute-start.12 = (bf16[4,16,2048]{2,1,0:T(8,128)(2,1)S(1)}, bf16[4,16,2048]{2,1,0:T(8,128)(2,1)S(1)}, u32[]{:S(2)}, u32[]{:S(2)}) collective-permute-start(bf16[4,16,2048]{2,1,0:T(8,128)(2,1)S(1)} %collective-permute-done.8.refs_1_), channel_id=1, source_target_pairs={{0,1},{1,0},{2,3},{3,2},{4,5},{5,4},{6,7},{7,6},{8,9},{9,8},{10,11... | collective-permute-start | bytes 786440 | tf_op jit(solution)/shard_map/ppermute | solution.py:31
  25.4 1.9 %collective-permute-start.7 = (bf16[64,2176]{1,0:T(8,128)(2,1)S(1)}, bf16[64,2176]{1,0:T(8,128)(2,1)S(1)}, u32[]{:S(2)}, u32[]{:S(2)}) collective-permute-start(bf16[64,2176]{1,0:T(8,128)(2,1)S(1)} %get-tuple-element.23), channel_id=1, source_target_pairs={{0,1},{1,0},{2,3},{3,2},{4,5},{5,4},{6,7},{7,6},{8,9},{9,8},{10,11... | collective-permute-start | bytes 835592 | tf_op jit(solution)/shard_map/ppermute | solution.py:31
  26.8 4.9 %collective-permute-start.13 = (bf16[64,2176]{1,0:T(8,128)(2,1)S(1)}, bf16[64,2176]{1,0:T(8,128)(2,1)S(1)}, u32[]{:S(2)}, u32[]{:S(2)}) collective-permute-start(bf16[64,2176]{1,0:T(8,128)(2,1)S(1)} %get-tuple-element.26), channel_id=1, source_target_pairs={{0,1},{1,0},{2,3},{3,2},{4,5},{5,4},{6,7},{7,6},{8,9},{9,8},{10,11... | collective-permute-start | bytes 835592 | tf_op jit(solution)/shard_map/ppermute | solution.py:31
  27.4 5.6 %collective-permute-start.10 = (bf16[32,2176]{1,0:T(8,128)(2,1)S(1)}, bf16[32,2176]{1,0:T(8,128)(2,1)S(1)}, u32[]{:S(2)}, u32[]{:S(2)}) collective-permute-start(bf16[32,2176]{1,0:T(8,128)(2,1)S(1)} %get-tuple-element.29), channel_id=1, source_target_pairs={{0,2},{1,13},{2,0},{3,15},{4,6},{5,9},{6,4},{7,11},{8,10},{9,5},{1... | collective-permute-start | bytes 417800 | tf_op jit(solution)/shard_map/ppermute | solution.py:27
  29.0 6.8 %collective-permute-start.9 = (bf16[32,2176]{1,0:T(8,128)(2,1)S(1)}, bf16[32,2176]{1,0:T(8,128)(2,1)S(1)}, u32[]{:S(2)}, u32[]{:S(2)}) collective-permute-start(bf16[32,2176]{1,0:T(8,128)(2,1)S(1)} %get-tuple-element.28), channel_id=1, source_target_pairs={{0,4},{1,9},{2,6},{3,11},{4,0},{5,13},{6,2},{7,15},{8,12},{9,1},{1... | collective-permute-start | bytes 417800 | tf_op jit(solution)/shard_map/ppermute | solution.py:27
  31.8 7.2 %collective-permute-start.14 = (bf16[32,2176]{1,0:T(8,128)(2,1)S(1)}, bf16[32,2176]{1,0:T(8,128)(2,1)S(1)}, u32[]{:S(2)}, u32[]{:S(2)}) collective-permute-start(bf16[32,2176]{1,0:T(8,128)(2,1)S(1)} %get-tuple-element.30), channel_id=1, source_target_pairs={{0,6},{1,11},{2,4},{3,9},{4,2},{5,15},{6,0},{7,13},{8,14},{9,3},{1... | collective-permute-start | bytes 417800 | tf_op jit(solution)/shard_map/ppermute | solution.py:27
  32.4 6.7 %collective-permute-start.15 = (bf16[32,2176]{1,0:T(8,128)(2,1)S(1)}, bf16[32,2176]{1,0:T(8,128)(2,1)S(1)}, u32[]{:S(2)}, u32[]{:S(2)}) collective-permute-start(bf16[32,2176]{1,0:T(8,128)(2,1)S(1)} %get-tuple-element.31), channel_id=1, source_target_pairs={{0,0},{1,15},{2,2},{3,13},{4,4},{5,11},{6,6},{7,9},{8,8},{9,7},{10... | collective-permute-start | bytes 417800 | tf_op jit(solution)/shard_map/ppermute | solution.py:27
  39.2 5.6 %collective-permute-start.16 = (f32[16,2176]{1,0:T(8,128)S(1)}, f32[16,2176]{1,0:T(8,128)S(1)}, u32[]{:S(2)}, u32[]{:S(2)}) collective-permute-start(f32[16,2176]{1,0:T(8,128)S(1)} %slice.46), channel_id=1, source_target_pairs={{0,1},{1,0},{2,3},{3,2},{4,5},{5,4},{6,7},{7,6},{8,9},{9,8},{10,11... | collective-permute-start | bytes 417800 | tf_op jit(solution)/shard_map/ppermute | solution.py:31
  44.8 6.3 %collective-permute-start.17 = (bf16[16,2048]{1,0:T(8,128)(2,1)S(1)}, bf16[16,2048]{1,0:T(8,128)(2,1)S(1)}, u32[]{:S(2)}, u32[]{:S(2)}) collective-permute-start(bf16[16,2048]{1,0:T(8,128)(2,1)S(1)} %slice.51), channel_id=1, source_target_pairs={{16,0},{17,1},{18,2},{19,3},{20,4},{21,5},{22,6},{23,7},{24,8},{25... | collective-permute-start | bytes 196616 | tf_op jit(solution)/shard_map/ppermute | solution.py:37
